TPU v7x, 128 devices: a whole 4x4x4 slice. The times are simulated.
128 devices in a mesh: batch: 8 (over y, core), tensor: 16 (over z, x).
Axes of the slice: x: 4, y: 4, z: 4, core: 2. Of those that a mesh axis runs over, the one named last changes fastest.
Arguments:
- tokens: bfloat16 [32768, 1024], P(('batch', 'tensor')), may hold values from -6 to 6
- gain_attn: float32 [1024], replicated, may hold values from 0.1 to 1.9
- w_qkv: bfloat16 [1024, 3072], P('batch', 'tensor'), may hold values from -0.1875 to 0.1875
- w_attn_out: bfloat16 [1024, 1024], P('batch', 'tensor'), may hold values from -0.1875 to 0.1875
- kv_cache: bfloat16 [1024, 128, 2048], P('batch', None, 'tensor'), may hold values from -192 to 192
- page_table: int32 [8, 128], P('batch'), may hold values from 0 to 127, each once within a row
- cached_lengths: int32 [32], P('batch'), may hold values from 1 to 4096, 32768 in all
- gain_moe: float32 [1024], replicated, may hold values from 0.1 to 1.9
- w_router: bfloat16 [1024, 16], replicated, may hold values from -0.1875 to 0.1875
- routes: int32 [32768, 2], P(('batch', 'tensor')), may hold values from 0 to 15, all different within a row; in each aligned block of 256 rows (0 to 255, 256 to 511, ...) at most 40 rows name the same one
- w_in: bfloat16 [16, 1024, 5632], P('tensor'), may hold values from -0.1875 to 0.1875
- w_out: bfloat16 [16, 2816, 1024], P('tensor'), may hold values from -0.109375 to 0.109375
Outputs:
- mixed: bfloat16 [32768, 1024], P(('batch', 'tensor'))
Inputs may be any that keep to these rules, and one draw needn't show every extreme that they name: `page_table`: each row lists all 128 pages of one batch index's pool once; local request r of that batch index reads its cached tokens from entries r * 32 to (r + 1) * 32 - 1 in order. `cached_lengths`: they sum to 32768. `routes`: a token's 2 experts differ; in the rows of one device (256 aligned rows) no expert is named by more than 40 rows, a bound that some block reaches.
All inputs are finite; a program needn't handle non-finite values. No bound on the sum of `cached_lengths` on one device may be relied on, other than what follows from the above.
Results may differ from a plain program's by a relative error of at most 0.012.
Values may be sent and summed in bfloat16 or wider, within the bound.
A program may use at most 128 MiB of HBM per device.

v0:
```python
import math

import jax
import jax.numpy as jnp
from jax import lax
from jax.sharding import PartitionSpec as P

HD = 64


EPSILON = 1e-06
NEGATIVE = -1e30
CONTRACT = (((1,), (1,)), ((), ()))


def rms_norm(values, gain):
    values = values.astype(jnp.float32)
    mean_square = jnp.mean(values * values, axis=-1, keepdims=True)
    return values * lax.rsqrt(mean_square + EPSILON) * gain


def head_attention(queries, cache_keys, cache_values, span_keys, span_values, length):
    span = queries.shape[0]
    cache_max = cache_keys.shape[0]
    scale = 1.0 / math.sqrt(queries.shape[1])
    keys = jnp.concatenate([cache_keys, span_keys], axis=0)
    values_all = jnp.concatenate([cache_values, span_values], axis=0)
    height = min(512, span)
    column = jnp.arange(cache_max + span, dtype=jnp.int32)

    def one_block(first):
        query_block = lax.dynamic_slice_in_dim(queries, first, height, 0)
        scores = (
            lax.dot_general(query_block, keys, CONTRACT, preferred_element_type=jnp.float32) * scale
        )
        line = first + jnp.arange(height, dtype=jnp.int32)
        visible = jnp.where(
            column[None, :] < cache_max,
            column[None, :] < length,
            column[None, :] - cache_max <= line[:, None],
        )
        scores = jnp.where(visible, scores, NEGATIVE)
        top_score = jnp.max(scores, axis=1, keepdims=True)
        weights = jnp.exp(scores - top_score)
        weights = (weights / jnp.sum(weights, axis=1, keepdims=True)).astype(jnp.bfloat16)
        return jnp.dot(weights, values_all, preferred_element_type=jnp.float32).astype(jnp.bfloat16)

    outcome = lax.map(one_block, jnp.arange(span // height, dtype=jnp.int32) * height)
    return outcome.reshape(span, queries.shape[1])


def body(
    tokens,
    gain_attn,
    w_qkv,
    w_attn_out,
    kv_cache,
    page_table,
    cached_lengths,
    gain_moe,
    w_router,
    routes,
    w_in,
    w_out,
):
    normed = rms_norm(tokens, gain_attn).astype(jnp.bfloat16)
    full_qkv, out_columns = (
        lax.all_gather(w_qkv, "batch", axis=0, tiled=True),
        lax.all_gather(w_attn_out, "batch", axis=0, tiled=True),
    )
    projected = jnp.dot(
        lax.all_gather(normed, "tensor", axis=0, tiled=True),
        full_qkv,
        preferred_element_type=jnp.float32,
    ).astype(jnp.bfloat16)
    requests = cached_lengths.shape[0]
    span = projected.shape[0] // requests
    local_heads = out_columns.shape[1] // HD
    per_request = kv_cache.shape[0] // requests

    def one_request(request):
        block = lax.dynamic_slice_in_dim(projected, request * span, span, 0)
        pages = lax.dynamic_slice_in_dim(page_table[0], request * per_request, per_request, 0)
        cached = kv_cache[pages].reshape(per_request * kv_cache.shape[1], kv_cache.shape[2])
        length = cached_lengths[request]
        outputs = [
            head_attention(
                block[:, 0:HD],
                cached[:, 0:HD],
                cached[:, HD : 2 * HD],
                block[:, HD : 2 * HD],
                block[:, 2 * HD : 3 * HD],
                length,
            )
        ]
        return jnp.concatenate(outputs, axis=1)

    attended = lax.map(one_request, jnp.arange(requests, dtype=jnp.int32)).reshape(
        projected.shape[0], local_heads * HD
    )
    rows_here = tokens.shape[0]
    portion = lax.slice_in_dim(attended, 0, rows_here * lax.axis_size("tensor"), axis=0)
    projection = lax.psum_scatter(
        lax.dot_general(portion, out_columns, CONTRACT, preferred_element_type=jnp.float32),
        "tensor",
        scatter_dimension=0,
        tiled=True,
    )
    state = tokens.astype(jnp.float32) + projection
    normed_moe = rms_norm(state, gain_moe).astype(jnp.bfloat16)
    logits = jnp.dot(normed_moe, w_router, preferred_element_type=jnp.float32)
    experts = w_router.shape[1]
    top_count = routes.shape[1]
    onehot = (routes[:, :, None] == jnp.arange(experts, dtype=jnp.int32)[None, None, :]).astype(
        jnp.int32
    )
    picked = jnp.sum(onehot.astype(jnp.float32) * logits[:, None, :], axis=2)
    squashed = jax.nn.sigmoid(picked)
    gates = squashed / jnp.sum(squashed, axis=1, keepdims=True)
    flat_hits = onehot.reshape(rows_here * top_count, experts)
    before = jnp.cumsum(flat_hits, axis=0) - flat_hits
    slots = jnp.sum(before * flat_hits, axis=1).reshape(rows_here, top_count)
    capacity = max(2, (5 * rows_here * top_count + 4 * experts - 1) // (4 * experts))
    position = routes * capacity + slots
    slot_ids = jnp.arange(experts * capacity, dtype=jnp.int32)
    placing = jnp.any(slot_ids[:, None, None] == position[None, :, :], axis=2).astype(jnp.bfloat16)
    buffer = jnp.dot(placing, normed_moe, preferred_element_type=jnp.float32).astype(jnp.bfloat16)
    lanes = lax.axis_size("tensor")
    buffer = buffer.reshape(lanes, w_in.shape[0], capacity, normed_moe.shape[1])
    width_ff = w_out.shape[1]
    inner = jnp.einsum(
        "sekd,edf->sekf",
        lax.all_to_all(buffer, "tensor", split_axis=0, concat_axis=0, tiled=True),
        w_in,
        preferred_element_type=jnp.float32,
    )
    active = (jax.nn.gelu(inner[..., :width_ff], approximate=True) * inner[..., width_ff:]).astype(
        jnp.bfloat16
    )
    results = jnp.einsum(
        "sekf,efd->sekd", active, w_out, preferred_element_type=jnp.float32
    ).astype(jnp.bfloat16)
    returned = lax.all_to_all(results, "tensor", split_axis=0, concat_axis=0, tiled=True).reshape(
        experts * capacity, normed_moe.shape[1]
    )
    mixed = state
    for rank in range(top_count):
        pick = (position[:, rank : rank + 1] == slot_ids[None, :]).astype(jnp.bfloat16)
        mixed = mixed + gates[:, rank : rank + 1] * jnp.dot(
            pick, returned, preferred_element_type=jnp.float32
        )
    return mixed.astype(jnp.bfloat16)


def solution(mesh):
    in_specs = (
        P(("batch", "tensor"), None),
        P(),
        P("batch", "tensor"),
        P("batch", "tensor"),
        P("batch", None, "tensor"),
        P("batch", None),
        P("batch"),
        P(),
        P(),
        P(("batch", "tensor"), None),
        P("tensor", None, None),
        P("tensor", None, None),
    )
    out_specs = P(("batch", "tensor"), None)
    return jax.shard_map(body, mesh=mesh, in_specs=in_specs, out_specs=out_specs, check_vma=False)
```

profile of v0, /device:TPU:0, one launch (start us, length us, event | category | flops | bytes accessed | tf_op | source)
XLA Modules:
  0.0 420.2 jit_solution(17453850326317034817)
XLA Ops:
  9.9 13.5 %all_gather.11 = bf16[1024,64]{0,1:T(8,128)(2,1)} all-gather(bf16[128,64]{0,1:T(8,128)(2,1)} %param.19), channel_id=1, replica_groups=mesh['batch'=8,'tensor'=16] {'batch'}, dimensions={0}, use_global_device_ids=true | all-gather | bytes 147456 | tf_op jit(solution)/shard_map/all_gather | solution.py:69
  23.4 11.9 %all_gather.10 = bf16[1024,192]{0,1:T(8,128)(2,1)S(1)} all-gather(bf16[128,192]{0,1:T(8,128)(2,1)} %param.18), channel_id=1, replica_groups=mesh['batch'=8,'tensor'=16] {'batch'}, dimensions={0}, use_global_device_ids=true | all-gather | bytes 442368 | tf_op jit(solution)/shard_map/all_gather | solution.py:68
  35.4 48.0 %all-gather.2.cloned.1.call-done = bf16[4096,1024]{1,0:T(8,128)(2,1)} async-done(((bf16[256,1024]{1,0:T(8,128)(2,1)}), bf16[4096,1024]{1,0:T(8,128)(2,1)}) %all-gather.2.cloned.1.call-update) | async-done | bytes 8388624 | tf_op jit(solution)/shard_map/all_gather | solution.py:72
  83.3 7.5 %convolution_convert_fusion = bf16[4096,192]{0,1:T(8,128)(2,1)} fusion(bf16[4096,1024]{1,0:T(8,128)(2,1)} %all-gather.2.cloned.1.call-done, bf16[1024,192]{0,1:T(8,128)(2,1)S(1)} %all_gather.10), kind=kOutput, calls=%fused_computation.40 | convolution fusion | flops 1611399168 | bytes 10354688 | tf_op jit(solution)/shard_map/dot_general | solution.py:71
  90.8 131.6 %while.34 = (s32[]{:T(128)}, bf16[4,1024,64]{2,1,0:T(8,128)(2,1)}, s32[4]{0:T(128)S(1)}, bf16[4096,192]{0,1:T(8,128)(2,1)}, s32[1,128]{1,0:T(1,128)S(1)}, /*inde...) while((s32[]{:T(128)}, bf16[4,1024,64]{2,1,0:T(8,128)(2,1)}, ...), condition=%wide.region_6.7_spmd, body=%wide.region_1.6_spmd.sunk | while | flops 699973248 | bytes 42679912 | solution.py:98
  94.4 2.9 gather_fusion
  100.7 22.3 %while.35 = (s32[]{:T(128)}, bf16[2,512,64]{1,2,0:T(8,128)(2,1)S(1)}, s32[]{:T(128)}, s32[2]{0:T(128)S(1)}, bf16[1024,64]{0,1:T(8,128)(2,1)S(1)}, /*index=5*/bf1...) while((s32[]{:T(128)}, ...), condition=%wide.region_5.5_spmd.clone.clone, body=%wide.region_2.4_spmd.clone.clone.sunk | while | flops 697350656 | bytes 33892512 | solution.py:48
  104.7 2.9 fusion.93
  109.2 2.6 fusion.95
  115.9 2.9 fusion.93
  127.2 2.9 gather_fusion
  133.5 22.3 %while.35 = (s32[]{:T(128)}, bf16[2,512,64]{1,2,0:T(8,128)(2,1)S(1)}, s32[]{:T(128)}, s32[2]{0:T(128)S(1)}, bf16[1024,64]{0,1:T(8,128)(2,1)S(1)}, /*index=5*/bf1...) while((s32[]{:T(128)}, ...), condition=%wide.region_5.5_spmd.clone.clone, body=%wide.region_2.4_spmd.clone.clone.sunk | while | flops 697350656 | bytes 33892512 | solution.py:48
  137.6 2.9 fusion.93
  142.0 2.6 fusion.95
  148.7 2.9 fusion.93
  153.2 2.6 fusion.95
  160.1 2.9 gather_fusion
  166.4 22.3 %while.35 = (s32[]{:T(128)}, bf16[2,512,64]{1,2,0:T(8,128)(2,1)S(1)}, s32[]{:T(128)}, s32[2]{0:T(128)S(1)}, bf16[1024,64]{0,1:T(8,128)(2,1)S(1)}, /*index=5*/bf1...) while((s32[]{:T(128)}, ...), condition=%wide.region_5.5_spmd.clone.clone, body=%wide.region_2.4_spmd.clone.clone.sunk | while | flops 697350656 | bytes 33892512 | solution.py:48
  170.4 2.9 fusion.93
  181.6 2.9 fusion.93
  193.0 2.9 gather_fusion
  199.2 22.3 %while.35 = (s32[]{:T(128)}, bf16[2,512,64]{1,2,0:T(8,128)(2,1)S(1)}, s32[]{:T(128)}, s32[2]{0:T(128)S(1)}, bf16[1024,64]{0,1:T(8,128)(2,1)S(1)}, /*index=5*/bf1...) while((s32[]{:T(128)}, ...), condition=%wide.region_5.5_spmd.clone.clone, body=%wide.region_2.4_spmd.clone.clone.sunk | while | flops 697350656 | bytes 33892512 | solution.py:48
  203.3 2.9 fusion.93
  207.7 2.6 fusion.95
  214.4 2.9 fusion.93
  222.5 9.3 %fusion.63 = f32[4096,1024]{1,0:T(8,128)} fusion(bf16[4096,64]{1,0:T(8,128)(2,1)} %bitcast.125, bf16[1024,64]{0,1:T(8,128)(2,1)S(1)} %copy-done.3), kind=kOutput, calls=%fused_computation.94 | convolution fusion | flops 536870912 | bytes 17432576 | tf_op jit(solution)/shard_map/dot_general | solution.py:104
  234.8 107.4 %reduce-scatter.2.cloned.1.call-done = f32[256,1024]{1,0:T(8,128)} async-done(((f32[4096,1024]{1,0:T(8,128)}), f32[256,1024]{1,0:T(8,128)}) %reduce-scatter.2.cloned.1.call-update) | async-done | bytes 1048592 | tf_op jit(solution)/shard_map/reduce_scatter | solution.py:103
  345.6 25.1 %all_to_all.10 = bf16[16,1,40,1024]{3,2,1,0:T(8,128)(2,1)S(1)} all-to-all(bf16[16,1,40,1024]{3,2,1,0:T(8,128)(2,1)S(1)} %bitcast.124), channel_id=1, replica_groups=mesh['batch'=8,'tensor'=16] {'tensor'}, dimensions={0} | all-to-all | bytes 2621440 | tf_op jit(solution)/shard_map/all_to_all | solution.py:133
  370.8 10.6 %fusion.11 = f32[16,1,40,5632]{3,2,0,1:T(8,128)S(1)} fusion(bf16[1,1024,5632]{2,1,0:T(8,128)(2,1)} %param.26, bf16[16,1,40,1024]{3,2,1,0:T(8,128)(2,1)S(1)} %all_to_all.10), kind=kOutput, calls=%fused_computation.28 | convolution fusion | flops 7381975040 | bytes 27262976 | tf_op jit(solution)/shard_map/sekd,edf->sekf/dot_general | solution.py:131
  381.4 6.2 %fusion.35 = bf16[16,1,40,1024]{3,2,1,0:T(8,128)(2,1)} fusion(bf16[1,2816,1024]{2,1,0:T(8,128)(2,1)S(1)} %bitcast.131, f32[16,1,40,5632]{3,2,0,1:T(8,128)S(1)} %fusion.11), kind=kOutput, calls=%fused_computation.50 | convolution fusion | flops 3709665280 | bytes 21495808 | tf_op jit(solution)/shard_map/sekf,efd->sekd/dot_general | solution.py:140
  387.6 3.8 all-to-all-start.1
  391.8 19.4 %all-to-all-done.1 = bf16[16,1,40,1024]{3,2,1,0:T(8,128)(2,1)S(1)} async-done(((bf16[16,1,40,1024]{3,2,1,0:T(8,128)(2,1)}), bf16[16,1,40,1024]{3,2,1,0:T(8,128)(2,1)S(1)}, u32[]{:S(2)}, u32[]{:S(2)}) %all-to-all-start.1) | async-done | bytes 1310752 | tf_op jit(solution)/shard_map/all_to_all | solution.py:143
  (167 shorter events, 70.1 us)
Async XLA Ops:
  6.5 385.0 %copy-start = (bf16[1024,16]{0,1:T(8,128)(2,1)S(1)}, bf16[1024,16]{0,1:T(8,128)(2,1)}, u32[]{:S(2)}) copy-start(bf16[1024,16]{0,1:T(8,128)(2,1)} %param.24) | copy-start | bytes 98308
  6.5 76.8 %all-gather.2.cloned.1.call-start = ((), (), s32[]{:S(2)}) async-start(), calls=%async_computation.3 | async-start | bytes 8912896 | tf_op jit(solution)/shard_map/all_gather | solution.py:72
  9.8 332.4 %reduce-scatter.2.cloned.1.call-start = ((), (), s32[]{:S(2)}) async-start(), calls=%async_computation.4 | async-start | bytes 17825792 | tf_op jit(solution)/shard_map/reduce_scatter | solution.py:103
  35.4 55.5 %copy-start.6 = (s32[1,128]{1,0:T(1,128)S(1)}, s32[1,128]{1,0:T(1,128)}, u32[]{:S(2)}) copy-start(s32[1,128]{1,0:T(1,128)} %param.21) | copy-start | bytes 1540
  35.4 55.5 %copy-start.7 = (s32[4]{0:T(128)S(1)}, s32[4]{0:T(128)}, u32[]{:S(2)}) copy-start(s32[4]{0:T(128)} %param.22) | copy-start | bytes 52
  90.8 131.6 %copy-start.3 = (bf16[1024,64]{0,1:T(8,128)(2,1)S(1)}, bf16[1024,64]{0,1:T(8,128)(2,1)}, u32[]{:S(2)}) copy-start(bf16[1024,64]{0,1:T(8,128)(2,1)} %all_gather.11) | copy-start | bytes 393220
  231.7 0.7 copy-start.4
  231.7 110.5 %copy-start.1 = (bf16[256,1024]{1,0:T(8,128)(2,1)S(1)}, bf16[256,1024]{1,0:T(8,128)(2,1)}, u32[]{:S(2)}) copy-start(bf16[256,1024]{1,0:T(8,128)(2,1)} %param.16) | copy-start | bytes 1572868
  231.7 112.0 %copy-start.5 = (f32[1024]{0:T(1024)S(1)}, f32[1024]{0:T(1024)}, u32[]{:S(2)}) copy-start(f32[1024]{0:T(1024)} %param.23) | copy-start | bytes 12292
  345.6 35.7 %slice-start = ((s8[5767168]{0:T(1024)(128)(4,1)}), s8[4194304]{0:T(1024)(128)(4,1)S(1)}, s32[]{:S(2)}) async-start(s8[5767168]{0:T(1024)(128)(4,1)} %bitcast.130), calls=%async_computation.5 | async-start | bytes 8388608
  370.8 10.6 %slice-start.1 = ((s8[5767168]{0:T(1024)(128)(4,1)}), s8[1572864]{0:T(1024)(128)(4,1)S(1)}, s32[]{:S(2)}) async-start(s8[5767168]{0:T(1024)(128)(4,1)} %bitcast.130), calls=%async_computation.6 | async-start | bytes 3145728
  387.6 24.2 %copy-start.2 = (f32[256,1024]{1,0:T(8,128)S(1)}, f32[256,1024]{1,0:T(8,128)}, u32[]{:S(2)}) copy-start(f32[256,1024]{1,0:T(8,128)} %reduce-scatter.2.cloned.1.call-done) | copy-start | bytes 3145732
  387.6 23.6 %all-to-all-start.1 = ((bf16[16,1,40,1024]{3,2,1,0:T(8,128)(2,1)}), bf16[16,1,40,1024]{3,2,1,0:T(8,128)(2,1)S(1)}, u32[]{:S(2)}, u32[]{:S(2)}) async-start(bf16[16,1,40,1024]{3,2,1,0:T(8,128)(2,1)} %fusion.35), calls=%async_computation.2 | async-start | bytes 2621440 | tf_op jit(solution)/shard_map/all_to_all | solution.py:143
Sparse Core Ops, SparseCore 0:
  10.0 73.3 all-gather.1
  231.9 110.3 reduce-scatter.1
where the time goes:
time: 421 us; the launch traced here: 420 us
  waiting for transfers between devices  175 us (42%)
  matrix products  80.5 us (19%)
  blocking collectives  50.6 us (12%)
  local copies, waits for them, and re-layouts  35.3 us (8%)
  other arithmetic  33 us (8%)
  loops' own time  28.5 us (7%)
  between operations  13.6 us (3%)
    reduce_scatter x1, waiting for transfers between devices, body(): lax.psum_scatter(lax.dot_general(portion, out_columns, CONTRACT, preferre...  107 us
    all_gather x1, waiting for transfers between devices, body(): lax.all_gather(normed, 'tensor', axis=0, tiled=True)  48 us
    all_to_all x1, blocking collectives, body(): lax.all_to_all(buffer, 'tensor', split_axis=0, concat_axis=0, tiled=True)  25.1 us
    dot_general x8, matrix products, one_block(): lax.dot_general(query_block, keys, CONTRACT, preferred_element_type=jnp.f...  22.9 us
    dot_general x8, matrix products, one_block(): jnp.dot(weights, values_all, preferred_element_type=jnp.float32)  21.2 us
    all_to_all x1, waiting for transfers between devices, body(): lax.all_to_all(results, 'tensor', split_axis=0, concat_axis=0, tiled=True)  19.4 us
    another operation x4, loops' own time, head_attention(): lax.map(one_block, jnp.arange(span // height, dtype=jnp.int32) * height)  15.7 us
    all_gather x1, blocking collectives, body(): lax.all_gather(w_attn_out, 'batch', axis=0, tiled=True)  13.5 us
  transfers between devices with their start and end apart: 3, of which 3 were waited for; matrix products, arithmetic and copies ran while one was open for 1% of the time, Pallas kernels for 0%

commit v1 on v0

v1 whole, which is shorter than its diff:
```python
import math

import jax
import jax.numpy as jnp
from jax import lax
from jax.experimental import pallas as pl
from jax.experimental.pallas import tpu as pltpu
from jax.sharding import PartitionSpec as P

HD = 64


EPSILON = 1e-06
NEGATIVE = -1e30
CONTRACT = (((1,), (1,)), ((), ()))


def rms_norm(values, gain):
    values = values.astype(jnp.float32)
    mean_square = jnp.mean(values * values, axis=-1, keepdims=True)
    return values * lax.rsqrt(mean_square + EPSILON) * gain


PAGE = 128
TQ = 256
CK = 512


def attention_kernel(table, lengths, q_ref, kv_ref, cache_ref, out_ref, pages, top, total, sems):
    requests, per_request = pages.shape[0], pages.shape[1] // PAGE
    span = q_ref.shape[0] // requests
    tiles = span // TQ

    def fetch(entry):
        return pltpu.make_async_copy(
            cache_ref.at[table[entry]],
            pages.at[entry // per_request, pl.ds((entry % per_request) * PAGE, PAGE), :],
            sems.at[entry],
        )

    @pl.loop(0, requests * per_request)
    def _(entry):
        fetch(entry).start()

    lane = lax.broadcasted_iota(jnp.int32, (CK, 128), 1)
    triangle = lax.broadcasted_iota(jnp.int32, (TQ, TQ), 1) <= lax.broadcasted_iota(
        jnp.int32, (TQ, TQ), 0
    )
    column = lax.broadcasted_iota(jnp.int32, (TQ, CK), 1)

    def with_ones(kv):
        return jnp.where(lane[: kv.shape[0]] < HD, jnp.ones_like(kv), kv)

    def scores_of(queries, kv):
        return lax.dot_general(queries, kv, CONTRACT, preferred_element_type=jnp.float32)

    def mix(weights, kv):
        return jnp.dot(weights.astype(jnp.bfloat16), with_ones(kv), preferred_element_type=jnp.float32)

    @pl.loop(0, requests)
    def _(request):
        base = pl.multiple_of(request * span, span)
        length = lengths[request]

        for tile in range(tiles):
            queries = q_ref[pl.ds(base + tile * TQ, TQ), :]
            own = kv_ref[pl.ds(base + tile * TQ, TQ), :]
            diagonal = jnp.where(triangle, scores_of(queries, own), NEGATIVE)
            high = jnp.max(diagonal, axis=1, keepdims=True)
            earlier = []
            for at in range(tile):
                block = kv_ref[pl.ds(base + at * TQ, TQ), :]
                scores = scores_of(queries, block)
                high = jnp.maximum(high, jnp.max(scores, axis=1, keepdims=True))
                earlier.append((block, scores))
            result = mix(jnp.exp(diagonal - high), own)
            for block, scores in earlier:
                result = result + mix(jnp.exp(scores - high), block)
            total[pl.ds(tile * TQ, TQ), :] = result
            top[pl.ds(tile * TQ, TQ), :] = jnp.broadcast_to(high, (TQ, 128))

        @pl.loop(0, per_request)
        def _(page):
            fetch(request * per_request + page).wait()

        def chunk(index, masked):
            first = pl.multiple_of(index * CK, CK)
            kv = pages[request, pl.ds(first, CK), :]
            values = with_ones(kv)
            for tile in range(tiles):
                rows = pl.ds(tile * TQ, TQ)
                scores = scores_of(q_ref[pl.ds(base + tile * TQ, TQ), :], kv)
                if masked:
                    scores = jnp.where(column < length - first, scores, NEGATIVE)
                old = top[rows, :]
                new = jnp.maximum(old, jnp.max(scores, axis=1, keepdims=True))
                weights = jnp.exp(scores - new[:, :1]).astype(jnp.bfloat16)
                total[rows, :] = total[rows, :] * jnp.exp(old - new) + jnp.dot(
                    weights, values, preferred_element_type=jnp.float32
                )
                top[rows, :] = new

        whole = length // CK

        @pl.loop(0, whole)
        def _(index):
            chunk(index, False)

        @pl.when(length % CK > 0)
        def _():
            chunk(whole, True)

        for tile in range(tiles):
            low = total[pl.ds(tile * TQ, TQ // 2), :]
            high = total[pl.ds(tile * TQ + TQ // 2, TQ // 2), :]
            side = lax.broadcasted_iota(jnp.int32, low.shape, 1) < HD
            low_out = pltpu.roll(low, HD, 1) / low
            high_out = high / pltpu.roll(high, HD, 1)
            out_ref[request * tiles + tile] = jnp.where(side, low_out, high_out).astype(jnp.bfloat16)


def attention(table, lengths, queries, kv, cache):
    rows = queries.shape[0]
    requests = lengths.shape[0]
    cached = table.shape[0] // requests * PAGE
    vmem = pl.BlockSpec(memory_space=pltpu.VMEM)
    smem = pl.BlockSpec(memory_space=pltpu.SMEM)
    return pl.pallas_call(
        attention_kernel,
        out_shape=jax.ShapeDtypeStruct((rows // TQ, TQ // 2, 2 * HD), jnp.bfloat16),
        in_specs=[smem, smem, vmem, vmem, pl.BlockSpec(memory_space=pl.ANY)],
        out_specs=vmem,
        scratch_shapes=[
            pltpu.VMEM((requests, cached, 2 * HD), jnp.bfloat16),
            pltpu.VMEM((rows // requests, 128), jnp.float32),
            pltpu.VMEM((rows // requests, 2 * HD), jnp.float32),
            pltpu.SemaphoreType.DMA((table.shape[0],)),
        ],
        cost_estimate=pl.CostEstimate(
            flops=4 * rows * 128 * 2560, bytes_accessed=8 << 20, transcendentals=rows * 2560
        ),
        compiler_params=pltpu.CompilerParams(vmem_limit_bytes=40 << 20),
        name="paged_attention",
    )(table, lengths, queries, kv, cache)


def body(
    tokens,
    gain_attn,
    w_qkv,
    w_attn_out,
    kv_cache,
    page_table,
    cached_lengths,
    gain_moe,
    w_router,
    routes,
    w_in,
    w_out,
):
    normed = rms_norm(tokens, gain_attn).astype(jnp.bfloat16)
    zeros = jnp.zeros((w_qkv.shape[0], HD), w_qkv.dtype)
    packed = jnp.concatenate([w_qkv[:, :HD] * 0.125, zeros, w_qkv[:, HD:]], axis=1)
    full_qkv = lax.all_gather(packed, "batch", axis=0, tiled=True)
    projected = jnp.dot(
        lax.all_gather(normed, "tensor", axis=0, tiled=True),
        full_qkv,
        preferred_element_type=jnp.float32,
    ).astype(jnp.bfloat16)
    out_weights = lax.all_gather(w_attn_out, ("batch", "tensor"), axis=0)
    lanes = lax.axis_size("tensor")
    out_weights = out_weights.reshape(-1, lanes, *w_attn_out.shape)
    rows_here = tokens.shape[0]
    attended = attention(
        page_table[0], cached_lengths, projected[:, : 2 * HD], projected[:, 2 * HD :], kv_cache
    )
    shares = lax.all_to_all(attended, "tensor", split_axis=0, concat_axis=0, tiled=True)
    shares = shares.reshape(lanes, TQ // 2, 2, HD).transpose(2, 1, 0, 3).reshape(rows_here, lanes * HD)
    out_weights = out_weights.transpose(0, 2, 1, 3).reshape(-1, lanes * HD)
    projection = lax.dot_general(shares, out_weights, CONTRACT, preferred_element_type=jnp.float32)
    state = tokens.astype(jnp.float32) + projection
    normed_moe = rms_norm(state, gain_moe).astype(jnp.bfloat16)
    logits = jnp.dot(normed_moe, w_router, preferred_element_type=jnp.float32)
    experts = w_router.shape[1]
    top_count = routes.shape[1]
    onehot = (routes[:, :, None] == jnp.arange(experts, dtype=jnp.int32)[None, None, :]).astype(
        jnp.int32
    )
    picked = jnp.sum(onehot.astype(jnp.float32) * logits[:, None, :], axis=2)
    squashed = jax.nn.sigmoid(picked)
    gates = squashed / jnp.sum(squashed, axis=1, keepdims=True)
    flat_hits = onehot.reshape(rows_here * top_count, experts)
    before = jnp.cumsum(flat_hits, axis=0) - flat_hits
    slots = jnp.sum(before * flat_hits, axis=1).reshape(rows_here, top_count)
    capacity = max(2, (5 * rows_here * top_count + 4 * experts - 1) // (4 * experts))
    position = routes * capacity + slots
    slot_ids = jnp.arange(experts * capacity, dtype=jnp.int32)
    placing = jnp.any(slot_ids[:, None, None] == position[None, :, :], axis=2).astype(jnp.bfloat16)
    buffer = jnp.dot(placing, normed_moe, preferred_element_type=jnp.float32).astype(jnp.bfloat16)
    buffer = buffer.reshape(lanes, w_in.shape[0], capacity, normed_moe.shape[1])
    width_ff = w_out.shape[1]
    inner = jnp.einsum(
        "sekd,edf->sekf",
        lax.all_to_all(buffer, "tensor", split_axis=0, concat_axis=0, tiled=True),
        w_in,
        preferred_element_type=jnp.float32,
    )
    active = (jax.nn.gelu(inner[..., :width_ff], approximate=True) * inner[..., width_ff:]).astype(
        jnp.bfloat16
    )
    results = jnp.einsum(
        "sekf,efd->sekd", active, w_out, preferred_element_type=jnp.float32
    ).astype(jnp.bfloat16)
    returned = lax.all_to_all(results, "tensor", split_axis=0, concat_axis=0, tiled=True).reshape(
        experts * capacity, normed_moe.shape[1]
    )
    mixed = state
    for rank in range(top_count):
        pick = (position[:, rank : rank + 1] == slot_ids[None, :]).astype(jnp.bfloat16)
        mixed = mixed + gates[:, rank : rank + 1] * jnp.dot(
            pick, returned, preferred_element_type=jnp.float32
        )
    return mixed.astype(jnp.bfloat16)


def solution(mesh):
    in_specs = (
        P(("batch", "tensor"), None),
        P(),
        P("batch", "tensor"),
        P("batch", "tensor"),
        P("batch", None, "tensor"),
        P("batch", None),
        P("batch"),
        P(),
        P(),
        P(("batch", "tensor"), None),
        P("tensor", None, None),
        P("tensor", None, None),
    )
    out_specs = P(("batch", "tensor"), None)
    return jax.shard_map(body, mesh=mesh, in_specs=in_specs, out_specs=out_specs, check_vma=False)
```

time: 421 us -> 236 us (0.56)
  waiting for transfers between devices: 175 us -> 82 us
  matrix products: 80.5 us -> 28 us
  Pallas kernels: 0 us -> 47.4 us
  loops' own time: 28.5 us -> 0 us
  other arithmetic: 33 us -> 5.7 us
  local copies, waits for them, and re-layouts: 35.3 us -> 9.46 us
  blocking collectives: 50.6 us -> 38.7 us
  starting transfers between devices: 3.88 us -> 9.02 us
    reduce_scatter x1 -> x0, waiting for transfers between devices: 107 us -> none  [body(): lax.psum_scatter(lax.dot_general(portion, out_columns, CONTRACT, preferre...]
    dot_general x17 -> x1, matrix products: 53.4 us -> 2.41 us  [body(): lax.dot_general(shares, out_weights, CONTRACT, preferred_element_type=jnp...]
    pallas_call x0 -> x1, Pallas kernels: none -> 47.4 us  [attention(): pl.pallas_call(attention_kernel, out_shape=jax.ShapeDtypeStruct((rows //...]
    another operation x5 -> x0, loops' own time: 28.5 us -> none  [the longest x4 15.7 us: head_attention(): lax.map(one_block, jnp.arange(span // height, dtype=jnp.int32) * height)]
    reduce_sum x8 -> x0, other arithmetic: 12.7 us -> none  [one_block(): jnp.sum(weights, axis=1, keepdims=True)]
    all_gather x2 -> x1, blocking collectives: 25.5 us -> 13 us  [body(): full_qkv = lax.all_gather(packed, 'batch', axis=0, tiled=True)]
    gather x4 -> x0, local copies, waits for them, and re-layouts: 11.7 us -> none  [one_request(): kv_cache[pages].reshape(per_request * kv_cache.shape[1], kv_cache.shape[2])]
    dynamic_slice x32 -> x0, local copies, waits for them, and re-layouts: 11.3 us -> none  [the longest x8 4.88 us: head_attention(): lax.map(one_block, jnp.arange(span // height, dtype=jnp.int32) * height)]
  transfers between devices with their start and end apart: 3 -> 4, of which waited for: 3 -> 3; matrix products, arithmetic and copies ran while one was open for 1% -> 6% of each run, Pallas kernels for 0% -> 20%
where the time goes in v1:
time: 236 us; the launch traced here: 234 us
  waiting for transfers between devices  82 us (35%)
  Pallas kernels  47.4 us (20%)
  blocking collectives  38.7 us (16%)
  matrix products  28 us (12%)
  between operations  13.7 us (6%)
  local copies, waits for them, and re-layouts  9.46 us (4%)
  starting transfers between devices  9.02 us (4%)
  other arithmetic  5.7 us (2%)
    all_gather x1, waiting for transfers between devices, body(): lax.all_gather(normed, 'tensor', axis=0, tiled=True)  55.9 us
    pallas_call x1, Pallas kernels, attention(): pl.pallas_call(attention_kernel, out_shape=jax.ShapeDtypeStruct((rows //...  47.4 us
    all_to_all x1, blocking collectives, body(): lax.all_to_all(buffer, 'tensor', split_axis=0, concat_axis=0, tiled=True)  25.7 us
    all_to_all x1, waiting for transfers between devices, body(): lax.all_to_all(results, 'tensor', split_axis=0, concat_axis=0, tiled=True)  19.9 us
    all_gather x1, blocking collectives, body(): full_qkv = lax.all_gather(packed, 'batch', axis=0, tiled=True)  13 us
    dot_general x1, matrix products, body(): jnp.einsum('sekd,edf->sekf', lax.all_to_all(buffer, 'tensor', split_axis=...  10.6 us
    dot_general x1, matrix products, body(): jnp.einsum('sekf,efd->sekd', active, w_out, preferred_element_type=jnp.fl...  6.23 us
    dot_general x1, matrix products, body(): jnp.dot(lax.all_gather(normed, 'tensor', axis=0, tiled=True), full_qkv, p...  5.77 us
  transfers between devices with their start and end apart: 4, of which 3 were waited for; matrix products, arithmetic and copies ran while one was open for 6% of the time, Pallas kernels for 20%

profile of v1, /device:TPU:0, one launch (start us, length us, event | category | flops | bytes accessed | tf_op | source)
XLA Modules:
  0.0 234.0 jit_solution(10064371469391065449)
XLA Ops:
  6.5 1.2 fusion.41
  7.8 2.0 fusion.43
  9.9 0.7 all-gather.6.cloned.1.call-update
  10.6 0.8 copy.62
  11.6 0.8 slice.37
  12.3 1.2 reduce-window.6
  13.6 0.7 slice_multiply_fusion
  14.4 13.0 %all_gather.13 = bf16[1024,256]{0,1:T(8,128)(2,1)S(1)} all-gather(bf16[128,256]{0,1:T(8,128)(2,1)S(1)} %pad_maximum_fusion), channel_id=1, replica_groups=mesh['batch'=8,'tensor'=16] {'batch'}, dimensions={0}, use_global_device_ids=true | all-gather | bytes 589824 | tf_op jit(solution)/shard_map/all_gather | solution.py:164
  27.4 55.9 %all-gather.4.cloned.1.call-done = bf16[4096,1024]{1,0:T(8,128)(2,1)} async-done(((bf16[256,1024]{1,0:T(8,128)(2,1)}), bf16[4096,1024]{1,0:T(8,128)(2,1)}) %all-gather.4.cloned.1.call-update) | async-done | bytes 8388624 | tf_op jit(solution)/shard_map/all_gather | solution.py:166
  83.3 5.8 %convolution_convert_fusion = bf16[4096,256]{1,0:T(8,128)(2,1)S(1)} fusion(bf16[4096,1024]{1,0:T(8,128)(2,1)} %all-gather.4.cloned.1.call-done, bf16[1024,256]{0,1:T(8,128)(2,1)S(1)} %all_gather.13), kind=kOutput, calls=%fused_computation.15 | convolution fusion | flops 2148532224 | bytes 11010048 | tf_op jit(solution)/shard_map/dot_general | solution.py:165
  89.3 2.0 copy-done.1
  91.3 47.4 %paged_attention.1 = bf16[16,128,128]{2,1,0:T(8,128)(2,1)} custom-call(s32[128]{0:T(128)S(1)} %bitcast.101, s32[4]{0:T(128)S(1)} %copy-done.3, bf16[4096,128]{1,0:T(8,128)(2,1)S(1)} %get-tuple-element.6.q_ref, bf16[4096,128]{1,0:T(8,128)(2,1)S(1)} %get-tuple-element.5.kv_ref, bf16[128,128,128]{2,1,0:T(8,128)(2,1)S(1)} %copy-done.1), custom_call_target="tpu_custom_call" | custom-call | flops 5368709120 | bytes 8388608 | tf_op jit(solution)/shard_map/paged_attention/pallas_call | solution.py:128
  138.7 5.3 %all-to-all-start = ((bf16[16,128,128]{2,1,0:T(8,128)(2,1)}), bf16[16,128,128]{2,1,0:T(8,128)(2,1)S(1)}, u32[]{:S(2)}, u32[]{:S(2)}) async-start(bf16[16,128,128]{2,1,0:T(8,128)(2,1)} %paged_attention.1), calls=%async_computation | async-start | bytes 1048576 | tf_op jit(solution)/shard_map/all_to_all | solution.py:177
  144.0 0.2 slice_reduce_fusion
  144.2 0.1 eq.78
  144.5 0.1 reshape.79
  144.7 0.2 fusion.39
  144.9 5.5 %all-gather.6.cloned.1.call-done = bf16[16384,64]{0,1:T(8,128)(2,1)} async-done(((bf16[128,64]{0,1:T(8,128)(2,1)}), bf16[16384,64]{0,1:T(8,128)(2,1)}) %all-gather.6.cloned.1.call-update) | async-done | bytes 2097168 | tf_op jit(solution)/shard_map/all_gather | solution.py:170
  150.4 2.2 copy.70
  152.6 1.9 copy.61
  154.5 0.3 copy.59
  154.8 0.5 copy.60
  155.4 2.4 %multiply_reduce_fusion = (f32[256]{0:T(256)S(1)}, f32[256,1024]{1,0:T(8,128)S(1)}) fusion(bf16[128,8,8,128]{3,2,1,0:T(8,128)(2,1)} %bitcast.107, bf16[128,8,2,128]{3,2,1,0:T(2,128)(2,1)S(1)} %bitcast.109, bf16[256,1024]{1,0:T(8,128)(2,1)S(1)} %copy-done.4), kind=kOutput, calls=%fused_computation.41 | convolution fusion | flops 537919232 | bytes 4195328 | tf_op jit(solution)/shard_map/dot_general | solution.py:180
  157.8 0.6 convolution_convert_fusion.1
  158.4 25.7 %all_to_all.15 = bf16[16,1,40,1024]{3,2,1,0:T(8,128)(2,1)S(1)} all-to-all(bf16[16,1,40,1024]{3,2,1,0:T(8,128)(2,1)S(1)} %bitcast.105), channel_id=1, replica_groups=mesh['batch'=8,'tensor'=16] {'tensor'}, dimensions={0} | all-to-all | bytes 2621440 | tf_op jit(solution)/shard_map/all_to_all | solution.py:204
  184.1 10.6 %fusion.2 = f32[16,1,40,5632]{3,2,0,1:T(8,128)S(1)} fusion(bf16[1,1024,5632]{2,1,0:T(8,128)(2,1)} %param.22, bf16[16,1,40,1024]{3,2,1,0:T(8,128)(2,1)S(1)} %all_to_all.15), kind=kOutput, calls=%fused_computation.3 | convolution fusion | flops 7381975040 | bytes 27262976 | tf_op jit(solution)/shard_map/sekd,edf->sekf/dot_general | solution.py:202
  194.7 6.2 %fusion.29 = bf16[16,1,40,1024]{3,2,1,0:T(8,128)(2,1)} fusion(bf16[1,2816,1024]{2,1,0:T(8,128)(2,1)S(1)} %bitcast.115, f32[16,1,40,5632]{3,2,0,1:T(8,128)S(1)} %fusion.2), kind=kOutput, calls=%fused_computation.28 | convolution fusion | flops 3709665280 | bytes 21495808 | tf_op jit(solution)/shard_map/sekf,efd->sekd/dot_general | solution.py:211
  201.0 3.7 %all-to-all-start.2 = ((bf16[16,1,40,1024]{3,2,1,0:T(8,128)(2,1)}), bf16[16,1,40,1024]{3,2,1,0:T(8,128)(2,1)S(1)}, u32[]{:S(2)}, u32[]{:S(2)}) async-start(bf16[16,1,40,1024]{3,2,1,0:T(8,128)(2,1)} %fusion.29), calls=%async_computation.2 | async-start | bytes 2621440 | tf_op jit(solution)/shard_map/all_to_all | solution.py:214
  204.7 0.3 fusion.56
  205.1 19.9 %all-to-all-done.2 = bf16[16,1,40,1024]{3,2,1,0:T(8,128)(2,1)S(1)} async-done(((bf16[16,1,40,1024]{3,2,1,0:T(8,128)(2,1)}), bf16[16,1,40,1024]{3,2,1,0:T(8,128)(2,1)S(1)}, u32[]{:S(2)}, u32[]{:S(2)}) %all-to-all-start.2) | async-done | bytes 1310752 | tf_op jit(solution)/shard_map/all_to_all | solution.py:214
  225.0 0.6 convolution_multiply_fusion
  225.6 1.5 fusion.40
  (40 shorter events, 0.9 us)
Async XLA Ops:
  6.5 198.2 %copy-start = (bf16[1024,16]{0,1:T(8,128)(2,1)S(1)}, bf16[1024,16]{0,1:T(8,128)(2,1)}, u32[]{:S(2)}) copy-start(bf16[1024,16]{0,1:T(8,128)(2,1)} %param.20) | copy-start | bytes 98308
  6.5 76.8 %all-gather.4.cloned.1.call-start = ((), (), s32[]{:S(2)}) async-start(), calls=%async_computation.3 | async-start | bytes 8912896 | tf_op jit(solution)/shard_map/all_gather | solution.py:166
  9.8 140.6 %all-gather.6.cloned.1.call-start = ((), (), s32[]{:S(2)}) async-start(), calls=%async_computation.4 | async-start | bytes 2113536 | tf_op jit(solution)/shard_map/all_gather | solution.py:170
  89.1 2.2 copy-start.1
  89.1 2.2 copy-start.2
  89.1 2.2 copy-start.3
  91.3 53.4 %copy-start.5 = (s32[256,2]{0,1:T(2,128)S(1)}, s32[256,2]{0,1:T(2,128)}, u32[]{:S(2)}) copy-start(s32[256,2]{0,1:T(2,128)} %param.21) | copy-start | bytes 6148
  138.7 15.8 %all-to-all-start = ((bf16[16,128,128]{2,1,0:T(8,128)(2,1)}), bf16[16,128,128]{2,1,0:T(8,128)(2,1)S(1)}, u32[]{:S(2)}, u32[]{:S(2)}) async-start(bf16[16,128,128]{2,1,0:T(8,128)(2,1)} %paged_attention.1), calls=%async_computation | async-start | bytes 1048576 | tf_op jit(solution)/shard_map/all_to_all | solution.py:177
  152.6 2.8 %copy-start.4 = (bf16[256,1024]{1,0:T(8,128)(2,1)S(1)}, bf16[256,1024]{1,0:T(8,128)(2,1)}, u32[]{:S(2)}) copy-start(bf16[256,1024]{1,0:T(8,128)(2,1)} %param.12) | copy-start | bytes 1572868
  154.5 3.3 %copy-start.6 = (f32[1024]{0:T(1024)S(1)}, f32[1024]{0:T(1024)}, u32[]{:S(2)}) copy-start(f32[1024]{0:T(1024)} %param.19) | copy-start | bytes 12292
  158.4 36.3 %slice-start = ((s8[5767168]{0:T(1024)(128)(4,1)}), s8[4194304]{0:T(1024)(128)(4,1)S(1)}, s32[]{:S(2)}) async-start(s8[5767168]{0:T(1024)(128)(4,1)} %bitcast.114), calls=%async_computation.5 | async-start | bytes 8388608
  184.1 10.6 %slice-start.1 = ((s8[5767168]{0:T(1024)(128)(4,1)}), s8[1572864]{0:T(1024)(128)(4,1)S(1)}, s32[]{:S(2)}) async-start(s8[5767168]{0:T(1024)(128)(4,1)} %bitcast.114), calls=%async_computation.6 | async-start | bytes 3145728
  201.0 24.0 %all-to-all-start.2 = ((bf16[16,1,40,1024]{3,2,1,0:T(8,128)(2,1)}), bf16[16,1,40,1024]{3,2,1,0:T(8,128)(2,1)S(1)}, u32[]{:S(2)}, u32[]{:S(2)}) async-start(bf16[16,1,40,1024]{3,2,1,0:T(8,128)(2,1)} %fusion.29), calls=%async_computation.2 | async-start | bytes 2621440 | tf_op jit(solution)/shard_map/all_to_all | solution.py:214
Sparse Core Ops, SparseCore 0:
  10.0 73.3 all-gather.3
  86.1 64.2 all-gather.5

commit v2 on v1

--- a/solution.py
+++ b/solution.py
@@ -26,10 +26,12 @@
 CK = 512
 
 
-def attention_kernel(table, lengths, q_ref, kv_ref, cache_ref, out_ref, pages, top, total, sems):
+def attention_kernel(
+    table, lengths, blocks_ref, cache_ref, out_ref, pages, q_ref, top, total, sems
+):
     requests, per_request = pages.shape[0], pages.shape[1] // PAGE
-    span = q_ref.shape[0] // requests
-    tiles = span // TQ
+    tiles = blocks_ref.shape[0] // requests
+    half = TQ // 2
 
     def fetch(entry):
         return pltpu.make_async_copy(
@@ -59,17 +61,23 @@
 
     @pl.loop(0, requests)
     def _(request):
-        base = pl.multiple_of(request * span, span)
         length = lengths[request]
-
+        left = lax.broadcasted_iota(jnp.int32, (half, 2 * HD), 1) < HD
         for tile in range(tiles):
-            queries = q_ref[pl.ds(base + tile * TQ, TQ), :]
-            own = kv_ref[pl.ds(base + tile * TQ, TQ), :]
+            both = blocks_ref[request * tiles + tile, pl.ds(0, half), :].astype(jnp.float32)
+            for part, queries in enumerate((both, pltpu.roll(both, HD, 1))):
+                q_ref[pl.ds(tile * TQ + part * half, half), :] = jnp.where(
+                    left, queries, 0.0
+                ).astype(jnp.bfloat16)
+
+        for tile in range(tiles):
+            queries = q_ref[pl.ds(tile * TQ, TQ), :]
+            own = blocks_ref[request * tiles + tile, pl.ds(half, TQ), :]
             diagonal = jnp.where(triangle, scores_of(queries, own), NEGATIVE)
             high = jnp.max(diagonal, axis=1, keepdims=True)
             earlier = []
             for at in range(tile):
-                block = kv_ref[pl.ds(base + at * TQ, TQ), :]
+                block = blocks_ref[request * tiles + at, pl.ds(half, TQ), :]
                 scores = scores_of(queries, block)
                 high = jnp.maximum(high, jnp.max(scores, axis=1, keepdims=True))
                 earlier.append((block, scores))
@@ -89,7 +97,7 @@
             values = with_ones(kv)
             for tile in range(tiles):
                 rows = pl.ds(tile * TQ, TQ)
-                scores = scores_of(q_ref[pl.ds(base + tile * TQ, TQ), :], kv)
+                scores = scores_of(q_ref[rows, :], kv)
                 if masked:
                     scores = jnp.where(column < length - first, scores, NEGATIVE)
                 old = top[rows, :]
@@ -119,8 +127,8 @@
             out_ref[request * tiles + tile] = jnp.where(side, low_out, high_out).astype(jnp.bfloat16)
 
 
-def attention(table, lengths, queries, kv, cache):
-    rows = queries.shape[0]
+def attention(table, lengths, blocks, cache):
+    rows = blocks.shape[0] * TQ
     requests = lengths.shape[0]
     cached = table.shape[0] // requests * PAGE
     vmem = pl.BlockSpec(memory_space=pltpu.VMEM)
@@ -128,10 +136,11 @@
     return pl.pallas_call(
         attention_kernel,
         out_shape=jax.ShapeDtypeStruct((rows // TQ, TQ // 2, 2 * HD), jnp.bfloat16),
-        in_specs=[smem, smem, vmem, vmem, pl.BlockSpec(memory_space=pl.ANY)],
+        in_specs=[smem, smem, vmem, pl.BlockSpec(memory_space=pl.ANY)],
         out_specs=vmem,
         scratch_shapes=[
             pltpu.VMEM((requests, cached, 2 * HD), jnp.bfloat16),
+            pltpu.VMEM((rows // requests, 2 * HD), jnp.bfloat16),
             pltpu.VMEM((rows // requests, 128), jnp.float32),
             pltpu.VMEM((rows // requests, 2 * HD), jnp.float32),
             pltpu.SemaphoreType.DMA((table.shape[0],)),
@@ -141,7 +150,176 @@
         ),
         compiler_params=pltpu.CompilerParams(vmem_limit_bytes=40 << 20),
         name="paged_attention",
-    )(table, lengths, queries, kv, cache)
+    )(table, lengths, blocks, cache)
+
+
+MESH = pl.DeviceIdType.MESH
+SIDE = 4
+
+
+def place():
+    batch, tensor = lax.axis_index("batch"), lax.axis_index("tensor")
+    return batch // 2, batch % 2, tensor // SIDE, tensor % SIDE
+
+
+def device(y, core, z, x):
+    return {"batch": (y % SIDE) * 2 + core % 2, "tensor": (z % SIDE) * SIDE + x % SIDE}
+
+
+def send(source, target, sems, at, to):
+    return pltpu.make_async_remote_copy(
+        src_ref=source,
+        dst_ref=target,
+        send_sem=sems.at[0, at],
+        recv_sem=sems.at[1, at],
+        device_id=to,
+        device_id_type=MESH,
+    )
+
+
+def project_kernel(
+    x_ref, gain_ref, w_ref, out_ref, others, shards, w_query, w_kv, normed, packs,
+    w_sems, core_sems, x_sems, z_sems, local_sems,
+):
+    y, core, z, x = place()
+    half = TQ // 2
+    around = [(dy, dz) for dy in range(SIDE) for dz in range(SIDE) if dy or dz]
+    partner = device(y, core + 1, z, x)
+    right, left = device(y, core, z, x + 1), device(y, core, z, x + SIDE - 1)
+
+    barrier = pltpu.get_barrier_semaphore()
+    peers = [device(y + dy, core, z + dz, x) for dy, dz in around] + [partner, right, left]
+    for peer in peers:
+        pl.semaphore_signal(barrier, inc=1, device_id=peer, device_id_type=MESH)
+    pl.semaphore_wait(barrier, len(peers))
+
+    w_copies = {}
+    for at, (dy, dz) in enumerate(around):
+        w_copies[dy, dz] = send(
+            w_ref, shards.at[core, y, z], w_sems, at, device(y + dy, core, z + dz, x)
+        )
+        w_copies[dy, dz].start()
+    first, second = pl.ds(0, half), pl.ds(half, half)
+    x_copies = [
+        send(x_ref.at[first], others.at[0, first], x_sems, 0, right),
+        send(x_ref.at[second], others.at[1, second], x_sems, 1, left),
+        send(x_ref.at[second], others.at[0, second], x_sems, 2, right),
+        send(x_ref.at[first], others.at[1, first], x_sems, 3, left),
+        send(others.at[0, first], others.at[2, first], x_sems, 4, right),
+        send(others.at[1, second], others.at[2, second], x_sems, 5, left),
+    ]
+    for copy in x_copies[:4]:
+        copy.start()
+    own = pltpu.make_async_copy(w_ref, shards.at[core, y, z], local_sems.at[0])
+    own.start()
+
+    def norm(values):
+        values = values.astype(jnp.float32)
+        mean_square = jnp.mean(values * values, axis=-1, keepdims=True)
+        normed[...] = (values * lax.rsqrt(mean_square + EPSILON) * gain_ref[...]).astype(jnp.bfloat16)
+
+    norm(x_ref[...])
+    own.wait()
+    core_copies = []
+    for dy in range(SIDE):
+        for dz in range(SIDE):
+            if dy or dz:
+                w_copies[dy, dz].wait_recv()
+        source = (y - dy + SIDE) % SIDE
+        copy = send(shards.at[core, source], shards.at[core, source], core_sems, dy, partner)
+        copy.start()
+        core_copies.append(copy)
+        if dy == 1:
+            x_copies[0].wait_recv()
+            x_copies[4].start()
+            x_copies[1].wait_recv()
+            x_copies[5].start()
+    for copy in core_copies:
+        copy.wait_recv()
+    for index in range(2 * SIDE):
+        lanes = pl.ds(index * 128, 128)
+        for head in range(SIDE):
+            w_query[pl.ds(head * HD, HD), lanes] = shards[index % 2, index // 2, head, pl.ds(0, HD), :]
+            w_kv[pl.ds(head * 2 * HD, 2 * HD), lanes] = shards[
+                index % 2, index // 2, head, pl.ds(HD, 2 * HD), :
+            ]
+
+    side = lax.broadcasted_iota(jnp.int32, (half, 2 * HD), 1) < HD
+    z_copies = []
+    for step, shift in enumerate((0, SIDE - 1, 1, 2)):
+        if step == 1:
+            x_copies[2].wait_recv()
+        if step == 2:
+            x_copies[3].wait_recv()
+        if step == 3:
+            x_copies[4].wait_recv()
+            x_copies[5].wait_recv()
+        if step:
+            norm(others[step - 1])
+        queries = lax.dot_general(
+            normed[...], w_query[...], CONTRACT, preferred_element_type=jnp.float32
+        ) * (1.0 / math.sqrt(HD))
+        kv = lax.dot_general(
+            normed[...], w_kv[...], CONTRACT, preferred_element_type=jnp.float32
+        ).astype(jnp.bfloat16)
+        for pair in range(SIDE // 2):
+            early = queries[:half, pair * 2 * HD : (pair + 1) * 2 * HD]
+            late = queries[half:, pair * 2 * HD : (pair + 1) * 2 * HD]
+            packs[step, 2 * pair, first, :] = jnp.where(
+                side, early, pltpu.roll(late, HD, 1)
+            ).astype(jnp.bfloat16)
+            packs[step, 2 * pair + 1, first, :] = jnp.where(
+                side, pltpu.roll(early, HD, 1), late
+            ).astype(jnp.bfloat16)
+        for head in range(SIDE):
+            packs[step, head, pl.ds(half, TQ), :] = kv[:, head * 2 * HD : (head + 1) * 2 * HD]
+        block = out_ref.at[z * SIDE + (x + shift) % SIDE]
+        for dz in (2, 1, 3):
+            copy = send(
+                packs.at[step, (z + dz) % SIDE], block, z_sems, step * 3 + dz - 1,
+                device(y, core, z + dz, x),
+            )
+            copy.start()
+            z_copies.append(copy)
+        copy = pltpu.make_async_copy(packs.at[step, z], block, local_sems.at[1 + step])
+        copy.start()
+        z_copies.append(copy)
+    for copy in z_copies:
+        copy.wait()
+    for copy in list(w_copies.values()) + x_copies + core_copies:
+        copy.wait_send()
+
+
+def project(tokens, gain, weights):
+    rows, width = tokens.shape
+    vmem = pl.BlockSpec(memory_space=pltpu.VMEM)
+    bf16 = jnp.bfloat16
+    return pl.pallas_call(
+        project_kernel,
+        out_shape=jax.ShapeDtypeStruct((SIDE * SIDE, 3 * TQ // 2, 2 * HD), bf16),
+        in_specs=[vmem] * 3,
+        out_specs=vmem,
+        scratch_shapes=[
+            pltpu.VMEM((3, rows, width), bf16),
+            pltpu.VMEM((2, SIDE, SIDE, *weights.shape), bf16),
+            pltpu.VMEM((SIDE * HD, width), bf16),
+            pltpu.VMEM((SIDE * 2 * HD, width), bf16),
+            pltpu.VMEM((rows, width), bf16),
+            pltpu.VMEM((SIDE, SIDE, 3 * TQ // 2, 2 * HD), bf16),
+            pltpu.SemaphoreType.DMA((2, 15)),
+            pltpu.SemaphoreType.DMA((2, SIDE)),
+            pltpu.SemaphoreType.DMA((2, 6)),
+            pltpu.SemaphoreType.DMA((2, 12)),
+            pltpu.SemaphoreType.DMA((1 + SIDE,)),
+        ],
+        cost_estimate=pl.CostEstimate(
+            flops=6 * SIDE * rows * width * HD * SIDE, bytes_accessed=8 << 20, transcendentals=0
+        ),
+        compiler_params=pltpu.CompilerParams(
+            collective_id=0, has_side_effects=True, vmem_limit_bytes=32 << 20
+        ),
+        name="gather_project",
+    )(tokens, gain, weights)
 
 
 def body(
@@ -158,26 +336,17 @@
     w_in,
     w_out,
 ):
-    normed = rms_norm(tokens, gain_attn).astype(jnp.bfloat16)
-    zeros = jnp.zeros((w_qkv.shape[0], HD), w_qkv.dtype)
-    packed = jnp.concatenate([w_qkv[:, :HD] * 0.125, zeros, w_qkv[:, HD:]], axis=1)
-    full_qkv = lax.all_gather(packed, "batch", axis=0, tiled=True)
-    projected = jnp.dot(
-        lax.all_gather(normed, "tensor", axis=0, tiled=True),
-        full_qkv,
-        preferred_element_type=jnp.float32,
-    ).astype(jnp.bfloat16)
-    out_weights = lax.all_gather(w_attn_out, ("batch", "tensor"), axis=0)
     lanes = lax.axis_size("tensor")
-    out_weights = out_weights.reshape(-1, lanes, *w_attn_out.shape)
     rows_here = tokens.shape[0]
-    attended = attention(
-        page_table[0], cached_lengths, projected[:, : 2 * HD], projected[:, 2 * HD :], kv_cache
-    )
+    out_weights = lax.all_gather(w_attn_out.T, ("batch", "tensor"), axis=0)
+    out_weights = out_weights.reshape(-1, lanes * HD, w_attn_out.shape[0])
+    blocks = project(tokens, gain_attn.reshape(1, -1), w_qkv.T)
+    attended = attention(page_table[0], cached_lengths, blocks, kv_cache)
     shares = lax.all_to_all(attended, "tensor", split_axis=0, concat_axis=0, tiled=True)
     shares = shares.reshape(lanes, TQ // 2, 2, HD).transpose(2, 1, 0, 3).reshape(rows_here, lanes * HD)
-    out_weights = out_weights.transpose(0, 2, 1, 3).reshape(-1, lanes * HD)
-    projection = lax.dot_general(shares, out_weights, CONTRACT, preferred_element_type=jnp.float32)
+    projection = jnp.einsum(
+        "tk,bkn->tbn", shares, out_weights, preferred_element_type=jnp.float32
+    ).reshape(rows_here, -1)
     state = tokens.astype(jnp.float32) + projection
     normed_moe = rms_norm(state, gain_moe).astype(jnp.bfloat16)
     logits = jnp.dot(normed_moe, w_router, preferred_element_type=jnp.float32)

time: 236 us -> 185 us (0.78)
  waiting for transfers between devices: 82 us -> 29.9 us
  Pallas kernels: 47.4 us -> 76.5 us
  blocking collectives: 38.7 us -> 23.2 us
  matrix products: 28 us -> 22.3 us
  other arithmetic: 5.7 us -> 1.6 us
    all_gather x2 -> x1, waiting for transfers between devices: 61.4 us -> 0.02 us  [body(): out_weights = lax.all_gather(w_attn_out.T, ('batch', 'tensor'), axis=0)]
    pallas_call x0 -> x1, Pallas kernels: none -> 40.1 us  [project(): pl.pallas_call(project_kernel, out_shape=jax.ShapeDtypeStruct((SIDE * SID...]
    all_gather x1 -> x0, blocking collectives: 13 us -> none  [body(): full_qkv = lax.all_gather(packed, 'batch', axis=0, tiled=True)]
    pallas_call x1, Pallas kernels: 47.4 us -> 36.4 us  [attention(): pl.pallas_call(attention_kernel, out_shape=jax.ShapeDtypeStruct((rows //...]
    all_to_all x1, waiting for transfers between devices: 0.01 us -> 10.1 us  [body(): lax.all_to_all(attended, 'tensor', split_axis=0, concat_axis=0, tiled=True)]
    dot_general x2 -> x1, matrix products: 8.18 us -> 2.47 us  [body(): jnp.einsum('tk,bkn->tbn', shares, out_weights, preferred_element_type=jnp...]
    dot_general x0 -> x1, local copies, waits for them, and re-layouts: none -> 3.93 us  [body(): jnp.einsum('tk,bkn->tbn', shares, out_weights, preferred_element_type=jnp...]
    all_to_all x1, blocking collectives: 25.7 us -> 23.2 us  [body(): lax.all_to_all(buffer, 'tensor', split_axis=0, concat_axis=0, tiled=True)]
  transfers between devices with their start and end apart: 4 -> 3, of which waited for: 3 -> 2; matrix products, arithmetic and copies ran while one was open for 6% -> 2% of each run, Pallas kernels for 20% -> 41%
where the time goes in v2:
time: 185 us
  Pallas kernels  76.5 us (41%)
  waiting for transfers between devices  29.9 us (16%)
  blocking collectives  23.2 us (13%)
  matrix products  22.3 us (12%)
  between operations  13.7 us (7%)
  starting transfers between devices  8.82 us (5%)
  local copies, waits for them, and re-layouts  8.56 us (5%)
    pallas_call x1, Pallas kernels, project(): pl.pallas_call(project_kernel, out_shape=jax.ShapeDtypeStruct((SIDE * SID...  40.1 us
    pallas_call x1, Pallas kernels, attention(): pl.pallas_call(attention_kernel, out_shape=jax.ShapeDtypeStruct((rows //...  36.4 us
    all_to_all x1, blocking collectives, body(): lax.all_to_all(buffer, 'tensor', split_axis=0, concat_axis=0, tiled=True)  23.2 us
    all_to_all x1, waiting for transfers between devices, body(): lax.all_to_all(results, 'tensor', split_axis=0, concat_axis=0, tiled=True)  19.1 us
    dot_general x1, matrix products, body(): jnp.einsum('sekd,edf->sekf', lax.all_to_all(buffer, 'tensor', split_axis=...  10.6 us
    all_to_all x1, waiting for transfers between devices, body(): lax.all_to_all(attended, 'tensor', split_axis=0, concat_axis=0, tiled=True)  10.1 us
    dot_general x1, matrix products, body(): jnp.einsum('sekf,efd->sekd', active, w_out, preferred_element_type=jnp.fl...  6.23 us
    all_to_all x1, starting transfers between devices, body(): lax.all_to_all(attended, 'tensor', split_axis=0, concat_axis=0, tiled=True)  5.11 us
  transfers between devices with their start and end apart: 3, of which 2 were waited for; matrix products, arithmetic and copies ran while one was open for 2% of the time, Pallas kernels for 41%

profile of v2, /device:TPU:0, one launch (start us, length us, event | category | flops | bytes accessed | tf_op | source)
XLA Modules:
  0.0 184.6 jit_solution(2130169883969945403)
XLA Ops:
  6.5 0.7 all-gather.3.cloned.1.call-update
  7.3 1.2 copy-done.2
  8.5 1.0 copy-done.4
  9.5 0.7 copy-done.5
  10.2 40.1 %gather_project.1.blocks_ref = bf16[16,384,128]{2,1,0:T(8,128)(2,1)S(1)} custom-call(bf16[256,1024]{1,0:T(8,128)(2,1)S(1)} %copy-done.2, f32[1,1024]{1,0:T(1,128)S(1)} %bitcast.91, bf16[192,128]{1,0:T(8,128)(2,1)S(1)} %bitcast.90), custom_call_target="tpu_custom_call" | custom-call | flops 1610612736 | bytes 8388608 | tf_op jit(solution)/shard_map/gather_project/pallas_call | solution.py:297
  50.3 36.4 %paged_attention.1 = bf16[16,128,128]{2,1,0:T(8,128)(2,1)} custom-call(s32[128]{0:T(128)S(1)} %bitcast.92, s32[4]{0:T(128)S(1)} %copy-done.7, bf16[16,384,128]{2,1,0:T(8,128)(2,1)S(1)} %gather_project.1.blocks_ref, bf16[128,128,128]{2,1,0:T(8,128)(2,1)S(1)} %copy-done.1), custom_call_target="tpu_custom_call" | custom-call | flops 5368709120 | bytes 8388608 | tf_op jit(solution)/shard_map/paged_attention/pallas_call | solution.py:136
  86.8 5.1 %all-to-all-start = ((bf16[16,128,128]{2,1,0:T(8,128)(2,1)}), bf16[16,128,128]{2,1,0:T(8,128)(2,1)S(1)}, u32[]{:S(2)}, u32[]{:S(2)}) async-start(bf16[16,128,128]{2,1,0:T(8,128)(2,1)} %paged_attention.1), calls=%async_computation | async-start | bytes 1048576 | tf_op jit(solution)/shard_map/all_to_all | solution.py:345
  91.9 0.1 copy.61
  92.1 0.1 eq.82
  92.2 1.2 reduce-window.6
  93.4 0.2 slice_reduce_fusion
  93.6 0.1 eq.78
  93.8 0.1 fusion.42
  93.9 0.1 reshape.72
  94.0 0.1 copy.64
  94.1 0.2 fusion.34
  94.3 10.1 %all-to-all-done = bf16[16,128,128]{2,1,0:T(8,128)(2,1)S(1)} async-done(((bf16[16,128,128]{2,1,0:T(8,128)(2,1)}), bf16[16,128,128]{2,1,0:T(8,128)(2,1)S(1)}, u32[]{:S(2)}, u32[]{:S(2)}) %all-to-all-start) | async-done | bytes 524320 | tf_op jit(solution)/shard_map/all_to_all | solution.py:345
  104.4 0.3 copy.58
  104.7 0.5 copy.59
  105.2 0.0 all-gather.3.cloned.1.call-done
  105.3 3.9 %copy.60 = bf16[8,128,1024]{2,1,0:T(8,128)(2,1)} copy(bf16[8,128,1024]{1,2,0:T(8,128)(2,1)} %bitcast.96) | data formatting | bytes 4194304 | tf_op jit(solution)/shard_map/tk,bkn->tbn/dot_general | solution.py:347
  109.2 2.5 %multiply_reduce_fusion = (f32[256]{0:T(256)S(1)}, f32[256,1024]{1,0:T(8,128)S(1)}) fusion(bf16[1024,1024]{1,0:T(8,128)(2,1)} %bitcast.97, bf16[128,8,2,128]{3,2,1,0:T(2,128)(2,1)S(1)} %bitcast.99, bf16[256,1024]{1,0:T(8,128)(2,1)S(1)} %copy-done.3), kind=kOutput, calls=%fused_computation.32 | convolution fusion | flops 537919232 | bytes 4195328 | tf_op jit(solution)/shard_map/tk,bkn->tbn/dot_general | solution.py:347
  111.7 0.6 convolution_convert_fusion
  112.3 0.0 slice-start
  112.3 23.2 %all_to_all.15 = bf16[16,1,40,1024]{3,2,1,0:T(8,128)(2,1)S(1)} all-to-all(bf16[16,1,40,1024]{3,2,1,0:T(8,128)(2,1)S(1)} %bitcast.95), channel_id=1, replica_groups=mesh['batch'=8,'tensor'=16] {'tensor'}, dimensions={0} | all-to-all | bytes 2621440 | tf_op jit(solution)/shard_map/all_to_all | solution.py:373
  135.6 10.6 %fusion.2 = f32[16,1,40,5632]{3,2,0,1:T(8,128)S(1)} fusion(bf16[1,1024,5632]{2,1,0:T(8,128)(2,1)} %param.22, bf16[16,1,40,1024]{3,2,1,0:T(8,128)(2,1)S(1)} %all_to_all.15), kind=kOutput, calls=%fused_computation.3 | convolution fusion | flops 7381975040 | bytes 27262976 | tf_op jit(solution)/shard_map/sekd,edf->sekf/dot_general | solution.py:371
  146.2 6.2 %fusion.26 = bf16[16,1,40,1024]{3,2,1,0:T(8,128)(2,1)} fusion(bf16[1,2816,1024]{2,1,0:T(8,128)(2,1)S(1)} %bitcast.106, f32[16,1,40,5632]{3,2,0,1:T(8,128)S(1)} %fusion.2), kind=kOutput, calls=%fused_computation.21 | convolution fusion | flops 3709665280 | bytes 21495808 | tf_op jit(solution)/shard_map/sekf,efd->sekd/dot_general | solution.py:380
  152.4 3.7 %all-to-all-start.2 = ((bf16[16,1,40,1024]{3,2,1,0:T(8,128)(2,1)}), bf16[16,1,40,1024]{3,2,1,0:T(8,128)(2,1)S(1)}, u32[]{:S(2)}, u32[]{:S(2)}) async-start(bf16[16,1,40,1024]{3,2,1,0:T(8,128)(2,1)} %fusion.26), calls=%async_computation.2 | async-start | bytes 2621440 | tf_op jit(solution)/shard_map/all_to_all | solution.py:383
  156.1 0.3 fusion.48
  156.6 19.1 %all-to-all-done.2 = bf16[16,1,40,1024]{3,2,1,0:T(8,128)(2,1)S(1)} async-done(((bf16[16,1,40,1024]{3,2,1,0:T(8,128)(2,1)}), bf16[16,1,40,1024]{3,2,1,0:T(8,128)(2,1)S(1)}, u32[]{:S(2)}, u32[]{:S(2)}) %all-to-all-start.2) | async-done | bytes 1310752 | tf_op jit(solution)/shard_map/all_to_all | solution.py:383
  175.7 0.6 convolution_multiply_fusion
  176.3 1.5 fusion.35
  (32 shorter events, 0.2 us)
Async XLA Ops:
  6.5 149.6 %copy-start = (bf16[1024,16]{0,1:T(8,128)(2,1)S(1)}, bf16[1024,16]{0,1:T(8,128)(2,1)}, u32[]{:S(2)}) copy-start(bf16[1024,16]{0,1:T(8,128)(2,1)} %param.20) | copy-start | bytes 98308
  6.5 43.8 %copy-start.6 = (s32[1,128]{1,0:T(1,128)S(1)}, s32[1,128]{1,0:T(1,128)}, u32[]{:S(2)}) copy-start(s32[1,128]{1,0:T(1,128)} %param.17) | copy-start | bytes 1540
  6.5 43.8 %copy-start.7 = (s32[4]{0:T(128)S(1)}, s32[4]{0:T(128)}, u32[]{:S(2)}) copy-start(s32[4]{0:T(128)} %lengths.1) | copy-start | bytes 52
  6.5 98.7 %all-gather.3.cloned.1.call-start = ((), (), s32[]{:S(2)}) async-start(), calls=%async_computation.3 | async-start | bytes 2113536 | tf_op jit(solution)/shard_map/all_gather | solution.py:341
  7.3 43.0 %copy-start.1 = (bf16[128,128,128]{2,1,0:T(8,128)(2,1)S(1)}, bf16[128,128,128]{2,1,0:T(8,128)(2,1)}, u32[]{:S(2)}) copy-start(bf16[128,128,128]{2,1,0:T(8,128)(2,1)} %cache_ref.1) | copy-start | bytes 12582916
  7.3 1.2 copy-start.2
  8.5 1.0 copy-start.4
  9.5 0.7 copy-start.5
  50.3 41.6 %copy-start.8 = (s32[256,2]{0,1:T(2,128)S(1)}, s32[256,2]{0,1:T(2,128)}, u32[]{:S(2)}) copy-start(s32[256,2]{0,1:T(2,128)} %param.21) | copy-start | bytes 6148
  86.8 22.4 %copy-start.3 = (bf16[256,1024]{1,0:T(8,128)(2,1)S(1)}, bf16[256,1024]{1,0:T(8,128)(2,1)}, u32[]{:S(2)}) copy-start(bf16[256,1024]{1,0:T(8,128)(2,1)} %x_ref.1) | copy-start | bytes 1572868
  86.8 17.6 %all-to-all-start = ((bf16[16,128,128]{2,1,0:T(8,128)(2,1)}), bf16[16,128,128]{2,1,0:T(8,128)(2,1)S(1)}, u32[]{:S(2)}, u32[]{:S(2)}) async-start(bf16[16,128,128]{2,1,0:T(8,128)(2,1)} %paged_attention.1), calls=%async_computation | async-start | bytes 1048576 | tf_op jit(solution)/shard_map/all_to_all | solution.py:345
  92.1 19.6 %copy-start.9 = (f32[1024]{0:T(1024)S(1)}, f32[1024]{0:T(1024)}, u32[]{:S(2)}) copy-start(f32[1024]{0:T(1024)} %param.19) | copy-start | bytes 12292
  112.3 33.9 %slice-start = ((s8[5767168]{0:T(1024)(128)(4,1)}), s8[4194304]{0:T(1024)(128)(4,1)S(1)}, s32[]{:S(2)}) async-start(s8[5767168]{0:T(1024)(128)(4,1)} %bitcast.105), calls=%async_computation.4 | async-start | bytes 8388608
  135.6 10.6 %slice-start.1 = ((s8[5767168]{0:T(1024)(128)(4,1)}), s8[1572864]{0:T(1024)(128)(4,1)S(1)}, s32[]{:S(2)}) async-start(s8[5767168]{0:T(1024)(128)(4,1)} %bitcast.105), calls=%async_computation.5 | async-start | bytes 3145728
  152.4 23.3 %all-to-all-start.2 = ((bf16[16,1,40,1024]{3,2,1,0:T(8,128)(2,1)}), bf16[16,1,40,1024]{3,2,1,0:T(8,128)(2,1)S(1)}, u32[]{:S(2)}, u32[]{:S(2)}) async-start(bf16[16,1,40,1024]{3,2,1,0:T(8,128)(2,1)} %fusion.26), calls=%async_computation.2 | async-start | bytes 2621440 | tf_op jit(solution)/shard_map/all_to_all | solution.py:383
Sparse Core Ops, SparseCore 0:
  10.3 68.6 all-gather.2

commit v3 on v2

--- a/solution.py
+++ b/solution.py
@@ -26,87 +26,87 @@
 CK = 512
 
 
-def attention_kernel(
-    table, lengths, blocks_ref, cache_ref, out_ref, pages, q_ref, top, total, sems
-):
-    requests, per_request = pages.shape[0], pages.shape[1] // PAGE
+def attention_kernel(table, lengths, blocks_ref, cache_ref, out_ref, q_ref, kv_ref, flipped, top, total):
+    requests = lengths.shape[0]
     tiles = blocks_ref.shape[0] // requests
+    per_request = table.shape[0] // requests
     half = TQ // 2
-
-    def fetch(entry):
-        return pltpu.make_async_copy(
-            cache_ref.at[table[entry]],
-            pages.at[entry // per_request, pl.ds((entry % per_request) * PAGE, PAGE), :],
-            sems.at[entry],
+    left = lax.broadcasted_iota(jnp.int32, (half, 2 * HD), 1) < HD
+    triangle = lax.broadcasted_iota(jnp.int32, (TQ, TQ), 0) <= lax.broadcasted_iota(
+        jnp.int32, (TQ, TQ), 1
+    )
+    line = lax.broadcasted_iota(jnp.int32, (CK, TQ), 0)
+    flipped[pl.ds(HD, 16), :] = jnp.ones((16, flipped.shape[1]), jnp.bfloat16)
+
+    def scores_of(kv, tile):
+        return lax.dot_general(
+            kv, q_ref[pl.ds(tile * TQ, TQ), :], CONTRACT, preferred_element_type=jnp.float32
         )
-
-    @pl.loop(0, requests * per_request)
-    def _(entry):
-        fetch(entry).start()
-
-    lane = lax.broadcasted_iota(jnp.int32, (CK, 128), 1)
-    triangle = lax.broadcasted_iota(jnp.int32, (TQ, TQ), 1) <= lax.broadcasted_iota(
-        jnp.int32, (TQ, TQ), 0
-    )
-    column = lax.broadcasted_iota(jnp.int32, (TQ, CK), 1)
-
-    def with_ones(kv):
-        return jnp.where(lane[: kv.shape[0]] < HD, jnp.ones_like(kv), kv)
-
-    def scores_of(queries, kv):
-        return lax.dot_general(queries, kv, CONTRACT, preferred_element_type=jnp.float32)
-
-    def mix(weights, kv):
-        return jnp.dot(weights.astype(jnp.bfloat16), with_ones(kv), preferred_element_type=jnp.float32)
 
     @pl.loop(0, requests)
     def _(request):
         length = lengths[request]
-        left = lax.broadcasted_iota(jnp.int32, (half, 2 * HD), 1) < HD
         for tile in range(tiles):
-            both = blocks_ref[request * tiles + tile, pl.ds(0, half), :].astype(jnp.float32)
+            block = blocks_ref[request * tiles + tile]
+            both = block[:half].astype(jnp.float32)
             for part, queries in enumerate((both, pltpu.roll(both, HD, 1))):
                 q_ref[pl.ds(tile * TQ + part * half, half), :] = jnp.where(
                     left, queries, 0.0
                 ).astype(jnp.bfloat16)
-
+            kv = block[half:]
+            kv_ref[pl.ds(tile * TQ, TQ), :] = kv
+            flipped[pl.ds(0, HD), pl.ds(tile * TQ, TQ)] = kv.T[HD:]
+
+        def start(tile):
+            earlier = scores_of(kv_ref[pl.ds(0, tile * TQ), :], tile) if tile else None
+            return earlier, scores_of(kv_ref[pl.ds(tile * TQ, TQ), :], tile)
+
+        ahead = start(0)
         for tile in range(tiles):
-            queries = q_ref[pl.ds(tile * TQ, TQ), :]
-            own = blocks_ref[request * tiles + tile, pl.ds(half, TQ), :]
-            diagonal = jnp.where(triangle, scores_of(queries, own), NEGATIVE)
-            high = jnp.max(diagonal, axis=1, keepdims=True)
-            earlier = []
-            for at in range(tile):
-                block = blocks_ref[request * tiles + at, pl.ds(half, TQ), :]
-                scores = scores_of(queries, block)
-                high = jnp.maximum(high, jnp.max(scores, axis=1, keepdims=True))
-                earlier.append((block, scores))
-            result = mix(jnp.exp(diagonal - high), own)
-            for block, scores in earlier:
-                result = result + mix(jnp.exp(scores - high), block)
-            total[pl.ds(tile * TQ, TQ), :] = result
-            top[pl.ds(tile * TQ, TQ), :] = jnp.broadcast_to(high, (TQ, 128))
-
-        @pl.loop(0, per_request)
-        def _(page):
-            fetch(request * per_request + page).wait()
+            earlier, diagonal = ahead
+            if tile + 1 < tiles:
+                ahead = start(tile + 1)
+            columns = pl.ds(tile * TQ, TQ)
+            diagonal = jnp.where(triangle, diagonal, NEGATIVE)
+            high = jnp.max(diagonal, axis=0, keepdims=True)
+            if tile:
+                high = jnp.maximum(high, jnp.max(earlier, axis=0, keepdims=True))
+            result = jnp.dot(
+                flipped[:, columns],
+                jnp.exp(diagonal - high).astype(jnp.bfloat16),
+                preferred_element_type=jnp.float32,
+            )
+            if tile:
+                result = result + jnp.dot(
+                    flipped[:, pl.ds(0, tile * TQ)],
+                    jnp.exp(earlier - high).astype(jnp.bfloat16),
+                    preferred_element_type=jnp.float32,
+                )
+            total[:, columns] = result
+            top[:, columns] = high
 
         def chunk(index, masked):
-            first = pl.multiple_of(index * CK, CK)
-            kv = pages[request, pl.ds(first, CK), :]
-            values = with_ones(kv)
+            pages = [
+                cache_ref[table[request * per_request + index * (CK // PAGE) + at]]
+                for at in range(CK // PAGE)
+            ]
+            kv = jnp.concatenate(pages, axis=0)
+            values = jnp.concatenate([kv.T[HD:], jnp.ones((16, CK), jnp.bfloat16)], axis=0)
+            ahead = scores_of(kv, 0)
             for tile in range(tiles):
-                rows = pl.ds(tile * TQ, TQ)
-                scores = scores_of(q_ref[rows, :], kv)
+                scores = ahead
+                if tile + 1 < tiles:
+                    ahead = scores_of(kv, tile + 1)
+                columns = pl.ds(tile * TQ, TQ)
                 if masked:
-                    scores = jnp.where(column < length - first, scores, NEGATIVE)
-                old = top[rows, :]
-                new = jnp.maximum(old, jnp.max(scores, axis=1, keepdims=True))
-                weights = jnp.exp(scores - new[:, :1]).astype(jnp.bfloat16)
-                total[rows, :] = total[rows, :] * jnp.exp(old - new) + jnp.dot(
-                    weights, values, preferred_element_type=jnp.float32
+                    scores = jnp.where(line < length - index * CK, scores, NEGATIVE)
+                old = top[:, columns]
+                new = jnp.maximum(old, jnp.max(scores, axis=0, keepdims=True))
+                weights = jnp.exp(scores - new).astype(jnp.bfloat16)
+                total[:, columns] = total[:, columns] * jnp.exp(old - new) + jnp.dot(
+                    values, weights, preferred_element_type=jnp.float32
                 )
-                top[rows, :] = new
+                top[:, columns] = new
 
         whole = length // CK
 
@@ -119,36 +119,34 @@
             chunk(whole, True)
 
         for tile in range(tiles):
-            low = total[pl.ds(tile * TQ, TQ // 2), :]
-            high = total[pl.ds(tile * TQ + TQ // 2, TQ // 2), :]
-            side = lax.broadcasted_iota(jnp.int32, low.shape, 1) < HD
-            low_out = pltpu.roll(low, HD, 1) / low
-            high_out = high / pltpu.roll(high, HD, 1)
-            out_ref[request * tiles + tile] = jnp.where(side, low_out, high_out).astype(jnp.bfloat16)
+            columns = pl.ds(tile * TQ, TQ)
+            ratio = total[pl.ds(0, HD), columns] / total[pl.ds(HD, 1), columns]
+            ratio = jnp.concatenate([ratio[:, :half], ratio[:, half:]], axis=0)
+            out_ref[request * tiles + tile] = ratio.T.astype(jnp.bfloat16)
 
 
 def attention(table, lengths, blocks, cache):
     rows = blocks.shape[0] * TQ
     requests = lengths.shape[0]
-    cached = table.shape[0] // requests * PAGE
+    span = rows // requests
     vmem = pl.BlockSpec(memory_space=pltpu.VMEM)
     smem = pl.BlockSpec(memory_space=pltpu.SMEM)
     return pl.pallas_call(
         attention_kernel,
         out_shape=jax.ShapeDtypeStruct((rows // TQ, TQ // 2, 2 * HD), jnp.bfloat16),
-        in_specs=[smem, smem, vmem, pl.BlockSpec(memory_space=pl.ANY)],
+        in_specs=[smem, smem, vmem, vmem],
         out_specs=vmem,
         scratch_shapes=[
-            pltpu.VMEM((requests, cached, 2 * HD), jnp.bfloat16),
-            pltpu.VMEM((rows // requests, 2 * HD), jnp.bfloat16),
-            pltpu.VMEM((rows // requests, 128), jnp.float32),
-            pltpu.VMEM((rows // requests, 2 * HD), jnp.float32),
-            pltpu.SemaphoreType.DMA((table.shape[0],)),
+            pltpu.VMEM((span, 2 * HD), jnp.bfloat16),
+            pltpu.VMEM((span, 2 * HD), jnp.bfloat16),
+            pltpu.VMEM((HD + 16, span), jnp.bfloat16),
+            pltpu.VMEM((1, span), jnp.float32),
+            pltpu.VMEM((HD + 16, span), jnp.float32),
         ],
         cost_estimate=pl.CostEstimate(
             flops=4 * rows * 128 * 2560, bytes_accessed=8 << 20, transcendentals=rows * 2560
         ),
-        compiler_params=pltpu.CompilerParams(vmem_limit_bytes=40 << 20),
+        compiler_params=pltpu.CompilerParams(vmem_limit_bytes=24 << 20),
         name="paged_attention",
     )(table, lengths, blocks, cache)
 

time: 185 us -> 166 us (0.90); the launches traced: 185 us -> 163 us
  Pallas kernels: 76.5 us -> 52.9 us
    pallas_call x1, Pallas kernels: 36.4 us -> 12.8 us  [attention(): pl.pallas_call(attention_kernel, out_shape=jax.ShapeDtypeStruct((rows //...]
  transfers between devices with their start and end apart: 3 -> 3, of which waited for: 2 -> 2; matrix products, arithmetic and copies ran while one was open for 2% -> 2% of each run, Pallas kernels for 41% -> 32%
where the time goes in v3:
time: 166 us; the launch traced here: 163 us
  Pallas kernels  52.9 us (32%)
  waiting for transfers between devices  31.4 us (19%)
  blocking collectives  24.2 us (15%)
  matrix products  22.3 us (13%)
  between operations  13.7 us (8%)
  starting transfers between devices  8.8 us (5%)
  local copies, waits for them, and re-layouts  8.56 us (5%)
    pallas_call x1, Pallas kernels, project(): pl.pallas_call(project_kernel, out_shape=jax.ShapeDtypeStruct((SIDE * SID...  40.1 us
    all_to_all x1, blocking collectives, body(): lax.all_to_all(buffer, 'tensor', split_axis=0, concat_axis=0, tiled=True)  24.2 us
    all_to_all x1, waiting for transfers between devices, body(): lax.all_to_all(results, 'tensor', split_axis=0, concat_axis=0, tiled=True)  19.9 us
    pallas_call x1, Pallas kernels, attention(): pl.pallas_call(attention_kernel, out_shape=jax.ShapeDtypeStruct((rows //...  12.8 us
    all_to_all x1, waiting for transfers between devices, body(): lax.all_to_all(attended, 'tensor', split_axis=0, concat_axis=0, tiled=True)  10.7 us
    dot_general x1, matrix products, body(): jnp.einsum('sekd,edf->sekf', lax.all_to_all(buffer, 'tensor', split_axis=...  10.6 us
    dot_general x1, matrix products, body(): jnp.einsum('sekf,efd->sekd', active, w_out, preferred_element_type=jnp.fl...  6.23 us
    all_to_all x1, starting transfers between devices, body(): lax.all_to_all(attended, 'tensor', split_axis=0, concat_axis=0, tiled=True)  5.1 us
  transfers between devices with their start and end apart: 3, of which 2 were waited for; matrix products, arithmetic and copies ran while one was open for 2% of the time, Pallas kernels for 32%

profile of v3, /device:TPU:0, one launch (start us, length us, event | category | flops | bytes accessed | tf_op | source)
XLA Modules:
  0.0 163.3 jit_solution(16191992208545648384)
XLA Ops:
  6.5 0.7 all-gather.3.cloned.1.call-update
  7.3 1.2 copy-done.2
  8.5 1.0 copy-done.4
  9.5 0.7 copy-done.5
  10.2 40.1 %gather_project.1.blocks_ref = bf16[16,384,128]{2,1,0:T(8,128)(2,1)S(1)} custom-call(bf16[256,1024]{1,0:T(8,128)(2,1)S(1)} %copy-done.2, f32[1,1024]{1,0:T(1,128)S(1)} %bitcast.91, bf16[192,128]{1,0:T(8,128)(2,1)S(1)} %bitcast.90), custom_call_target="tpu_custom_call" | custom-call | flops 1610612736 | bytes 8388608 | tf_op jit(solution)/shard_map/gather_project/pallas_call | solution.py:295
  50.3 12.8 %paged_attention.1 = bf16[16,128,128]{2,1,0:T(8,128)(2,1)} custom-call(s32[128]{0:T(128)S(1)} %bitcast.92, s32[4]{0:T(128)S(1)} %copy-done.7, bf16[16,384,128]{2,1,0:T(8,128)(2,1)S(1)} %gather_project.1.blocks_ref, bf16[128,128,128]{2,1,0:T(8,128)(2,1)S(1)} %copy-done.1), custom_call_target="tpu_custom_call" | custom-call | flops 5368709120 | bytes 8388608 | tf_op jit(solution)/shard_map/paged_attention/pallas_call | solution.py:134
  63.1 5.1 %all-to-all-start = ((bf16[16,128,128]{2,1,0:T(8,128)(2,1)}), bf16[16,128,128]{2,1,0:T(8,128)(2,1)S(1)}, u32[]{:S(2)}, u32[]{:S(2)}) async-start(bf16[16,128,128]{2,1,0:T(8,128)(2,1)} %paged_attention.1), calls=%async_computation | async-start | bytes 1048576 | tf_op jit(solution)/shard_map/all_to_all | solution.py:343
  68.2 0.1 copy.61
  68.4 0.1 eq.82
  68.5 1.2 reduce-window.6
  69.7 0.2 slice_reduce_fusion
  69.9 0.1 eq.78
  70.1 0.1 fusion.42
  70.2 0.1 reshape.72
  70.3 0.1 copy.64
  70.4 0.2 fusion.34
  70.7 10.7 %all-to-all-done = bf16[16,128,128]{2,1,0:T(8,128)(2,1)S(1)} async-done(((bf16[16,128,128]{2,1,0:T(8,128)(2,1)}), bf16[16,128,128]{2,1,0:T(8,128)(2,1)S(1)}, u32[]{:S(2)}, u32[]{:S(2)}) %all-to-all-start) | async-done | bytes 524320 | tf_op jit(solution)/shard_map/all_to_all | solution.py:343
  81.4 0.3 copy.58
  81.7 0.5 copy.59
  82.2 0.0 all-gather.3.cloned.1.call-done
  82.3 3.9 %copy.60 = bf16[8,128,1024]{2,1,0:T(8,128)(2,1)} copy(bf16[8,128,1024]{1,2,0:T(8,128)(2,1)} %bitcast.96) | data formatting | bytes 4194304 | tf_op jit(solution)/shard_map/tk,bkn->tbn/dot_general | solution.py:345
  86.2 2.5 %multiply_reduce_fusion = (f32[256]{0:T(256)S(1)}, f32[256,1024]{1,0:T(8,128)S(1)}) fusion(bf16[1024,1024]{1,0:T(8,128)(2,1)} %bitcast.97, bf16[128,8,2,128]{3,2,1,0:T(2,128)(2,1)S(1)} %bitcast.99, bf16[256,1024]{1,0:T(8,128)(2,1)S(1)} %copy-done.3), kind=kOutput, calls=%fused_computation.32 | convolution fusion | flops 537919232 | bytes 4195328 | tf_op jit(solution)/shard_map/tk,bkn->tbn/dot_general | solution.py:345
  88.7 0.6 convolution_convert_fusion
  89.3 0.0 slice-start
  89.3 24.2 %all_to_all.15 = bf16[16,1,40,1024]{3,2,1,0:T(8,128)(2,1)S(1)} all-to-all(bf16[16,1,40,1024]{3,2,1,0:T(8,128)(2,1)S(1)} %bitcast.95), channel_id=1, replica_groups=mesh['batch'=8,'tensor'=16] {'tensor'}, dimensions={0} | all-to-all | bytes 2621440 | tf_op jit(solution)/shard_map/all_to_all | solution.py:371
  113.5 10.6 %fusion.2 = f32[16,1,40,5632]{3,2,0,1:T(8,128)S(1)} fusion(bf16[1,1024,5632]{2,1,0:T(8,128)(2,1)} %param.22, bf16[16,1,40,1024]{3,2,1,0:T(8,128)(2,1)S(1)} %all_to_all.15), kind=kOutput, calls=%fused_computation.3 | convolution fusion | flops 7381975040 | bytes 27262976 | tf_op jit(solution)/shard_map/sekd,edf->sekf/dot_general | solution.py:369
  124.1 6.2 %fusion.26 = bf16[16,1,40,1024]{3,2,1,0:T(8,128)(2,1)} fusion(bf16[1,2816,1024]{2,1,0:T(8,128)(2,1)S(1)} %bitcast.106, f32[16,1,40,5632]{3,2,0,1:T(8,128)S(1)} %fusion.2), kind=kOutput, calls=%fused_computation.21 | convolution fusion | flops 3709665280 | bytes 21495808 | tf_op jit(solution)/shard_map/sekf,efd->sekd/dot_general | solution.py:378
  130.3 3.7 %all-to-all-start.2 = ((bf16[16,1,40,1024]{3,2,1,0:T(8,128)(2,1)}), bf16[16,1,40,1024]{3,2,1,0:T(8,128)(2,1)S(1)}, u32[]{:S(2)}, u32[]{:S(2)}) async-start(bf16[16,1,40,1024]{3,2,1,0:T(8,128)(2,1)} %fusion.26), calls=%async_computation.2 | async-start | bytes 2621440 | tf_op jit(solution)/shard_map/all_to_all | solution.py:381
  134.1 0.3 fusion.48
  134.5 19.9 %all-to-all-done.2 = bf16[16,1,40,1024]{3,2,1,0:T(8,128)(2,1)S(1)} async-done(((bf16[16,1,40,1024]{3,2,1,0:T(8,128)(2,1)}), bf16[16,1,40,1024]{3,2,1,0:T(8,128)(2,1)S(1)}, u32[]{:S(2)}, u32[]{:S(2)}) %all-to-all-start.2) | async-done | bytes 1310752 | tf_op jit(solution)/shard_map/all_to_all | solution.py:381
  154.4 0.6 convolution_multiply_fusion
  155.0 1.5 fusion.35
  (32 shorter events, 0.2 us)
Async XLA Ops:
  6.5 127.5 %copy-start = (bf16[1024,16]{0,1:T(8,128)(2,1)S(1)}, bf16[1024,16]{0,1:T(8,128)(2,1)}, u32[]{:S(2)}) copy-start(bf16[1024,16]{0,1:T(8,128)(2,1)} %param.20) | copy-start | bytes 98308
  6.5 43.8 %copy-start.6 = (s32[1,128]{1,0:T(1,128)S(1)}, s32[1,128]{1,0:T(1,128)}, u32[]{:S(2)}) copy-start(s32[1,128]{1,0:T(1,128)} %param.17) | copy-start | bytes 1540
  6.5 43.8 %copy-start.7 = (s32[4]{0:T(128)S(1)}, s32[4]{0:T(128)}, u32[]{:S(2)}) copy-start(s32[4]{0:T(128)} %lengths.1) | copy-start | bytes 52
  6.5 75.7 %all-gather.3.cloned.1.call-start = ((), (), s32[]{:S(2)}) async-start(), calls=%async_computation.3 | async-start | bytes 2113536 | tf_op jit(solution)/shard_map/all_gather | solution.py:339
  7.3 43.0 %copy-start.1 = (bf16[128,128,128]{2,1,0:T(8,128)(2,1)S(1)}, bf16[128,128,128]{2,1,0:T(8,128)(2,1)}, u32[]{:S(2)}) copy-start(bf16[128,128,128]{2,1,0:T(8,128)(2,1)} %cache_ref.1) | copy-start | bytes 12582916
  7.3 1.2 copy-start.2
  8.5 1.0 copy-start.4
  9.5 0.7 copy-start.5
  50.3 17.9 %copy-start.8 = (s32[256,2]{0,1:T(2,128)S(1)}, s32[256,2]{0,1:T(2,128)}, u32[]{:S(2)}) copy-start(s32[256,2]{0,1:T(2,128)} %param.21) | copy-start | bytes 6148
  63.1 23.1 %copy-start.3 = (bf16[256,1024]{1,0:T(8,128)(2,1)S(1)}, bf16[256,1024]{1,0:T(8,128)(2,1)}, u32[]{:S(2)}) copy-start(bf16[256,1024]{1,0:T(8,128)(2,1)} %x_ref.1) | copy-start | bytes 1572868
  63.1 18.3 %all-to-all-start = ((bf16[16,128,128]{2,1,0:T(8,128)(2,1)}), bf16[16,128,128]{2,1,0:T(8,128)(2,1)S(1)}, u32[]{:S(2)}, u32[]{:S(2)}) async-start(bf16[16,128,128]{2,1,0:T(8,128)(2,1)} %paged_attention.1), calls=%async_computation | async-start | bytes 1048576 | tf_op jit(solution)/shard_map/all_to_all | solution.py:343
  68.4 20.3 %copy-start.9 = (f32[1024]{0:T(1024)S(1)}, f32[1024]{0:T(1024)}, u32[]{:S(2)}) copy-start(f32[1024]{0:T(1024)} %param.19) | copy-start | bytes 12292
  89.3 34.8 %slice-start = ((s8[5767168]{0:T(1024)(128)(4,1)}), s8[4194304]{0:T(1024)(128)(4,1)S(1)}, s32[]{:S(2)}) async-start(s8[5767168]{0:T(1024)(128)(4,1)} %bitcast.105), calls=%async_computation.4 | async-start | bytes 8388608
  113.5 10.6 %slice-start.1 = ((s8[5767168]{0:T(1024)(128)(4,1)}), s8[1572864]{0:T(1024)(128)(4,1)S(1)}, s32[]{:S(2)}) async-start(s8[5767168]{0:T(1024)(128)(4,1)} %bitcast.105), calls=%async_computation.5 | async-start | bytes 3145728
  130.3 24.0 %all-to-all-start.2 = ((bf16[16,1,40,1024]{3,2,1,0:T(8,128)(2,1)}), bf16[16,1,40,1024]{3,2,1,0:T(8,128)(2,1)S(1)}, u32[]{:S(2)}, u32[]{:S(2)}) async-start(bf16[16,1,40,1024]{3,2,1,0:T(8,128)(2,1)} %fusion.26), calls=%async_computation.2 | async-start | bytes 2621440 | tf_op jit(solution)/shard_map/all_to_all | solution.py:381
Sparse Core Ops, SparseCore 0:
  10.3 69.8 all-gather.2
